TPU v7x, 32 devices: a whole 2x2x4 slice. The times are simulated.
32 devices in a mesh: dp: 4 (over z), seq: 4 (over x, core), mp: 2 (over y).
Axes of the slice: x: 2, y: 2, z: 4, core: 2. Of those that a mesh axis runs over, the one named last changes fastest.
Arguments:
- tokens: bfloat16 [4, 1024, 1536], P('dp', 'seq'), may hold values from -6 to 6
- doc_lengths: int32 [4, 8], P('dp'), may hold values from 1 to 512, 1024 in all within a row
- attention_gain: float32 [1536], replicated, may hold values from 0.5 to 1.5
- query_weight: bfloat16 [1536, 1536], P(('dp', 'seq'), 'mp'), may hold values from -0.15625 to 0.15625
- key_weight: bfloat16 [1536, 1536], P(('dp', 'seq'), 'mp'), may hold values from -0.15625 to 0.15625
- value_weight: bfloat16 [1536, 1536], P(('dp', 'seq'), 'mp'), may hold values from -0.15625 to 0.15625
- output_weight: bfloat16 [1536, 1536], P(('dp', 'seq'), 'mp'), may hold values from -0.15625 to 0.15625
- head_gain: float32 [128], replicated, may hold values from 0.5 to 1.5
- lambda_vectors: float32 [4, 64], replicated, may hold values from -0.05 to 0.05
- feedforward_gain: float32 [1536], replicated, may hold values from 0.5 to 1.5
- gate_weight: bfloat16 [1536, 4096], P(('dp', 'seq'), 'mp'), may hold values from -0.15625 to 0.15625
- up_weight: bfloat16 [1536, 4096], P(('dp', 'seq'), 'mp'), may hold values from -0.15625 to 0.15625
- down_weight: bfloat16 [1536, 4096], P(('dp', 'seq'), 'mp'), may hold values from -0.09375 to 0.09375
- cotangent: bfloat16 [4, 1024, 1536], P('dp', 'seq'), may hold values from -6 to 6
Outputs:
- result: bfloat16 [4, 1024, 1536], P('dp', 'seq')
- tokens_grad: bfloat16 [4, 1024, 1536], P('dp', 'seq')
- attention_gain_grad: float32 [1536], replicated
- query_weight_grad: float32 [1536, 1536], P(('dp', 'seq'), 'mp')
- key_weight_grad: float32 [1536, 1536], P(('dp', 'seq'), 'mp')
- value_weight_grad: float32 [1536, 1536], P(('dp', 'seq'), 'mp')
- output_weight_grad: float32 [1536, 1536], P(('dp', 'seq'), 'mp')
- head_gain_grad: float32 [128], replicated
- lambda_grad: float32 [4, 64], replicated
- feedforward_gain_grad: float32 [1536], replicated
- gate_weight_grad: float32 [1536, 4096], P(('dp', 'seq'), 'mp')
- up_weight_grad: float32 [1536, 4096], P(('dp', 'seq'), 'mp')
- down_weight_grad: float32 [1536, 4096], P(('dp', 'seq'), 'mp')
Inputs may be any that keep to these rules, and one draw needn't show every extreme that they name: `doc_lengths`: each row's 8 entries are the lengths of its consecutive documents in order and sum to 1024; the last entry is the padding at the row's end.
All inputs are finite; a program needn't handle non-finite values.
Results may differ from a plain program's by a relative error of at most 0.015.
Values may be sent and summed in bfloat16 or wider, within the bound.
No kernel may reach another device: no remote copies, remote signals or barrier semaphores. Data moves between devices by JAX's collectives and lax.ppermute only.
A program may use at most 192 MiB of HBM per device.

v0:
```python
import math

import jax
import jax.numpy as jnp
from jax import lax
from jax.sharding import PartitionSpec as P

EPSILON = 1e-05
LAMBDA_INIT = 0.2
OUTPUT_SCALE = 1.0 - LAMBDA_INIT
NEGATIVE = -1e30


def tables(doc_lengths, length):
    doc_count = doc_lengths.shape[0]
    doc_ends = jnp.cumsum(doc_lengths)
    places = jnp.arange(length, dtype=jnp.int32)
    segment = jnp.sum((places[:, None] >= doc_ends[None, :]).astype(jnp.int32), axis=1)
    matched = segment[:, None] == jnp.arange(doc_count, dtype=jnp.int32)[None, :]
    doc_start = jnp.sum(jnp.where(matched, (doc_ends - doc_lengths)[None, :], 0), axis=1)
    return (segment, places - doc_start, segment < doc_count - 1)


def rotary(position, half_width):
    pair_count = half_width // 2
    frequency = jnp.exp(
        jnp.arange(pair_count, dtype=jnp.float32) * (-2.0 * math.log(10000.0) / half_width)
    )
    angles = position.astype(jnp.float32)[:, None] * frequency[None, :]
    return (jnp.cos(angles), jnp.sin(angles))


def rotate(values, cos_table, sin_table):
    middle = values.shape[-1] // 2
    first_half = values[..., :middle]
    second_half = values[..., middle:]
    return jnp.concatenate(
        [
            first_half * cos_table - second_half * sin_table,
            second_half * cos_table + first_half * sin_table,
        ],
        axis=-1,
    )


def rotate_back(values, cos_table, sin_table):
    middle = values.shape[-1] // 2
    first_half = values[..., :middle]
    second_half = values[..., middle:]
    return jnp.concatenate(
        [
            first_half * cos_table + second_half * sin_table,
            second_half * cos_table - first_half * sin_table,
        ],
        axis=-1,
    )


def norm_back(grad_normed, unit_values, inverse, gain):
    return inverse * (
        gain * grad_normed
        - unit_values * jnp.mean(gain * grad_normed * unit_values, axis=-1, keepdims=True)
    )


def head_forward(element, allowed, score_scale):
    query_pair, key_pair, value_head = element
    outputs = []
    logsums = []
    for half_index in range(2):
        scores = (
            jnp.einsum(
                "qd,kd->qk",
                query_pair[half_index],
                key_pair[half_index],
                preferred_element_type=jnp.float32,
            )
            * score_scale
        )
        scores = jnp.where(allowed, scores, NEGATIVE)
        highest = jnp.max(scores, axis=-1, keepdims=True)
        exponent = jnp.exp(scores - highest)
        row_total = jnp.sum(exponent, axis=-1, keepdims=True)
        weights_soft = exponent / row_total
        outputs.append(
            jnp.dot(
                weights_soft.astype(jnp.bfloat16), value_head, preferred_element_type=jnp.float32
            )
        )
        logsums.append((highest + jnp.log(row_total))[:, 0])
    return (outputs[0], outputs[1], jnp.stack(logsums))


def head_backward(element, allowed, score_scale):
    query_pair, key_pair, value_head, logsum_pair, grad_pair = element
    query_grads = []
    key_grads = []
    value_grad = jnp.zeros(value_head.shape, jnp.float32)
    for half_index in range(2):
        scores = (
            jnp.einsum(
                "qd,kd->qk",
                query_pair[half_index],
                key_pair[half_index],
                preferred_element_type=jnp.float32,
            )
            * score_scale
        )
        weights_soft = jnp.where(allowed, jnp.exp(scores - logsum_pair[half_index][:, None]), 0.0)
        grad_soft = jnp.einsum(
            "qe,ke->qk", grad_pair[half_index], value_head, preferred_element_type=jnp.float32
        )
        centre = jnp.sum(grad_soft * weights_soft, axis=-1, keepdims=True)
        grad_scores = (score_scale * weights_soft * (grad_soft - centre)).astype(jnp.bfloat16)
        query_grads.append(
            jnp.dot(grad_scores, key_pair[half_index], preferred_element_type=jnp.float32)
        )
        key_grads.append(
            jnp.einsum(
                "qk,qd->kd", grad_scores, query_pair[half_index], preferred_element_type=jnp.float32
            )
        )
        value_grad = value_grad + jnp.einsum(
            "qk,qe->ke",
            weights_soft.astype(jnp.bfloat16),
            grad_pair[half_index],
            preferred_element_type=jnp.float32,
        )
    return (jnp.stack(query_grads), jnp.stack(key_grads), value_grad)


def per_device(
    tokens,
    doc_lengths,
    attention_gain,
    query_weight,
    key_weight,
    value_weight,
    output_weight,
    head_gain,
    lambda_vectors,
    feedforward_gain,
    gate_weight,
    up_weight,
    down_weight,
    cotangent,
):
    local_len = tokens.shape[1]
    row_len = local_len * lax.axis_size("seq")
    offset = lax.axis_index("seq") * local_len
    segment, position, usable = tables(doc_lengths[0], row_len)
    places = jnp.arange(row_len, dtype=jnp.int32)
    local_segment = lax.dynamic_slice_in_dim(segment, offset, local_len)
    local_position = lax.dynamic_slice_in_dim(position, offset, local_len)
    local_usable = lax.dynamic_slice_in_dim(usable, offset, local_len)
    local_places = lax.dynamic_slice_in_dim(places, offset, local_len)
    allowed = (local_segment[:, None] == segment[None, :]) & (
        local_places[:, None] >= places[None, :]
    )
    half_width = lambda_vectors.shape[1]
    score_scale = half_width ** (-0.5)
    head_count = query_weight.shape[1] // (2 * half_width)
    full_weights = (
        lax.all_gather(query_weight, ("dp", "seq"), axis=0, tiled=True),
        lax.all_gather(key_weight, ("dp", "seq"), axis=0, tiled=True),
        lax.all_gather(value_weight, ("dp", "seq"), axis=0, tiled=True),
        lax.all_gather(output_weight, ("dp", "seq"), axis=0, tiled=True),
        lax.all_gather(gate_weight, ("dp", "seq"), axis=0, tiled=True),
        lax.all_gather(up_weight, ("dp", "seq"), axis=0, tiled=True),
        lax.all_gather(down_weight, ("dp", "seq"), axis=0, tiled=True),
    )
    query_full, key_full, value_full, output_full, gate_full, up_full, down_full = full_weights
    first_exp = jnp.exp(jnp.sum(lambda_vectors[0] * lambda_vectors[1]))
    second_exp = jnp.exp(jnp.sum(lambda_vectors[2] * lambda_vectors[3]))
    lam_value = first_exp - second_exp + LAMBDA_INIT
    inputs_f = tokens[0].astype(jnp.float32)
    inverse_one = lax.rsqrt(jnp.mean(inputs_f * inputs_f, axis=-1, keepdims=True) + EPSILON)
    unit_one = inputs_f * inverse_one
    normed_one = (unit_one * attention_gain).astype(jnp.bfloat16)
    cos_table, sin_table = rotary(local_position, half_width)
    cos_table = cos_table[:, None, :]
    sin_table = sin_table[:, None, :]
    query_rows = jnp.dot(normed_one, query_full, preferred_element_type=jnp.float32).reshape(
        local_len, 2 * head_count, half_width
    )
    query_rows = (
        rotate(query_rows, cos_table, sin_table)
        .astype(jnp.bfloat16)
        .reshape(local_len, 2 * head_count * half_width)
    )
    key_rows = jnp.dot(normed_one, key_full, preferred_element_type=jnp.float32).reshape(
        local_len, 2 * head_count, half_width
    )
    key_rows = (
        rotate(key_rows, cos_table, sin_table)
        .astype(jnp.bfloat16)
        .reshape(local_len, 2 * head_count * half_width)
    )
    value_rows = jnp.dot(normed_one, value_full, preferred_element_type=jnp.float32).astype(
        jnp.bfloat16
    )
    key_all, value_all = (
        lax.all_gather(key_rows, "seq", axis=0, tiled=True),
        lax.all_gather(value_rows, "seq", axis=0, tiled=True),
    )
    query_heads = jnp.transpose(
        query_rows.reshape(local_len, head_count, 2, half_width), (1, 2, 0, 3)
    )
    key_heads = jnp.transpose(key_all.reshape(row_len, head_count, 2, half_width), (1, 2, 0, 3))
    value_heads = jnp.transpose(value_all.reshape(row_len, head_count, 2 * half_width), (1, 0, 2))
    first_out, second_out, logsums = lax.map(
        lambda element: head_forward(element, allowed, score_scale),
        (query_heads, key_heads, value_heads),
    )
    mixture = first_out - lam_value * second_out
    inverse_head = lax.rsqrt(jnp.mean(mixture * mixture, axis=-1, keepdims=True) + EPSILON)
    unit_head = mixture * inverse_head
    head_scale = head_gain * OUTPUT_SCALE
    normed_head = (unit_head * head_scale).astype(jnp.bfloat16)
    flattened = jnp.transpose(normed_head, (1, 0, 2)).reshape(
        local_len, 2 * head_count * half_width
    )
    attention_part = jnp.einsum(
        "lx,dx->ld", flattened, output_full, preferred_element_type=jnp.float32
    )
    hidden_state = inputs_f + lax.psum(attention_part, "mp")
    inverse_two = lax.rsqrt(jnp.mean(hidden_state * hidden_state, axis=-1, keepdims=True) + EPSILON)
    unit_two = hidden_state * inverse_two
    normed_two = (unit_two * feedforward_gain).astype(jnp.bfloat16)
    gate_value = jnp.dot(normed_two, gate_full, preferred_element_type=jnp.float32)
    up_value = jnp.dot(normed_two, up_full, preferred_element_type=jnp.float32)
    gate_sigmoid = jax.nn.sigmoid(gate_value)
    gate_silu = gate_value * gate_sigmoid
    inner_act = (gate_silu * up_value).astype(jnp.bfloat16)
    feed_part = jnp.einsum("lf,df->ld", inner_act, down_full, preferred_element_type=jnp.float32)
    result = hidden_state + lax.psum(feed_part.astype(jnp.bfloat16), "mp").astype(jnp.float32)
    grad_out = cotangent[0].astype(jnp.float32) * local_usable[:, None].astype(jnp.float32)
    grad_out_low = grad_out.astype(jnp.bfloat16)
    down_grad = jnp.einsum("ld,lf->df", grad_out_low, inner_act, preferred_element_type=jnp.float32)
    grad_inner = jnp.dot(grad_out_low, down_full, preferred_element_type=jnp.float32)
    silu_slope = gate_sigmoid * (1.0 + gate_value * (1.0 - gate_sigmoid))
    grad_gate = (grad_inner * up_value * silu_slope).astype(jnp.bfloat16)
    grad_up = (grad_inner * gate_silu).astype(jnp.bfloat16)
    gate_grad = jnp.einsum("ld,lf->df", normed_two, grad_gate, preferred_element_type=jnp.float32)
    up_grad = jnp.einsum("ld,lf->df", normed_two, grad_up, preferred_element_type=jnp.float32)
    grad_two = jnp.einsum(
        "lf,df->ld", grad_gate, gate_full, preferred_element_type=jnp.float32
    ) + jnp.einsum("lf,df->ld", grad_up, up_full, preferred_element_type=jnp.float32)
    feed_gain_part = jnp.sum(grad_two * unit_two, axis=0)
    grad_hidden = grad_out + lax.psum(
        norm_back(grad_two, unit_two, inverse_two, feedforward_gain), "mp"
    )
    grad_hidden_low = grad_hidden.astype(jnp.bfloat16)
    output_grad = jnp.einsum(
        "ld,lx->dx", grad_hidden_low, flattened, preferred_element_type=jnp.float32
    )
    grad_flat = jnp.dot(grad_hidden_low, output_full, preferred_element_type=jnp.float32)
    grad_head = jnp.transpose(grad_flat.reshape(local_len, head_count, 2 * half_width), (1, 0, 2))
    head_gain_part = jnp.sum(grad_head * unit_head, axis=(0, 1)) * OUTPUT_SCALE
    grad_mixture = norm_back(grad_head, unit_head, inverse_head, head_scale)
    lambda_part = -jnp.sum(grad_mixture * second_out)
    grad_pair = jnp.stack(
        [grad_mixture.astype(jnp.bfloat16), (-lam_value * grad_mixture).astype(jnp.bfloat16)],
        axis=1,
    )
    query_back, key_back, value_back = lax.map(
        lambda element: head_backward(element, allowed, score_scale),
        (query_heads, key_heads, value_heads, logsums, grad_pair),
    )
    grad_query = jnp.transpose(query_back, (2, 0, 1, 3)).reshape(
        local_len, 2 * head_count, half_width
    )
    grad_query = (
        rotate_back(grad_query, cos_table, sin_table)
        .astype(jnp.bfloat16)
        .reshape(local_len, 2 * head_count * half_width)
    )
    key_row_grad = jnp.transpose(key_back, (2, 0, 1, 3)).reshape(
        row_len, 2 * head_count * half_width
    )
    value_row_grad = jnp.transpose(value_back, (1, 0, 2)).reshape(
        row_len, 2 * head_count * half_width
    )
    key_sum, value_sum = (
        lax.psum_scatter(
            key_row_grad.astype(jnp.bfloat16), "seq", scatter_dimension=0, tiled=True
        ).astype(jnp.float32),
        lax.psum_scatter(
            value_row_grad.astype(jnp.bfloat16), "seq", scatter_dimension=0, tiled=True
        ).astype(jnp.float32),
    )
    grad_key = rotate_back(
        key_sum.reshape(local_len, 2 * head_count, half_width), cos_table, sin_table
    )
    grad_key = grad_key.astype(jnp.bfloat16).reshape(local_len, 2 * head_count * half_width)
    grad_value = value_sum.astype(jnp.bfloat16)
    query_grad = jnp.einsum("ld,lx->dx", normed_one, grad_query, preferred_element_type=jnp.float32)
    key_grad = jnp.einsum("ld,lx->dx", normed_one, grad_key, preferred_element_type=jnp.float32)
    value_weight_grad = jnp.einsum(
        "ld,lx->dx", normed_one, grad_value, preferred_element_type=jnp.float32
    )
    grad_one = (
        jnp.einsum("lx,dx->ld", grad_query, query_full, preferred_element_type=jnp.float32)
        + jnp.einsum("lx,dx->ld", grad_key, key_full, preferred_element_type=jnp.float32)
        + jnp.einsum("lx,dx->ld", grad_value, value_full, preferred_element_type=jnp.float32)
    )
    attention_gain_part = jnp.sum(grad_one * unit_one, axis=0)
    grad_tokens = grad_hidden + lax.psum(
        norm_back(grad_one, unit_one, inverse_one, attention_gain).astype(jnp.bfloat16), "mp"
    ).astype(jnp.float32)
    gain_sums = lax.psum(
        (attention_gain_part, head_gain_part, lambda_part, feed_gain_part), ("dp", "seq", "mp")
    )
    lambda_total = gain_sums[2]
    lambda_grad = jnp.stack(
        [
            lambda_total * first_exp * lambda_vectors[1],
            lambda_total * first_exp * lambda_vectors[0],
            -lambda_total * second_exp * lambda_vectors[3],
            -lambda_total * second_exp * lambda_vectors[2],
        ]
    )
    weight_shards = (
        lax.psum_scatter(query_grad, ("dp", "seq"), scatter_dimension=0, tiled=True),
        lax.psum_scatter(key_grad, ("dp", "seq"), scatter_dimension=0, tiled=True),
        lax.psum_scatter(value_weight_grad, ("dp", "seq"), scatter_dimension=0, tiled=True),
        lax.psum_scatter(output_grad, ("dp", "seq"), scatter_dimension=0, tiled=True),
        lax.psum_scatter(gate_grad, ("dp", "seq"), scatter_dimension=0, tiled=True),
        lax.psum_scatter(up_grad, ("dp", "seq"), scatter_dimension=0, tiled=True),
        lax.psum_scatter(down_grad, ("dp", "seq"), scatter_dimension=0, tiled=True),
    )
    return (
        result.astype(jnp.bfloat16)[None],
        grad_tokens.astype(jnp.bfloat16)[None],
        gain_sums[0],
        weight_shards[0],
        weight_shards[1],
        weight_shards[2],
        weight_shards[3],
        gain_sums[1],
        lambda_grad,
        gain_sums[3],
        weight_shards[4],
        weight_shards[5],
        weight_shards[6],
    )


def solution(mesh):
    in_specs = (
        P("dp", "seq", None),
        P("dp", None),
        P(),
        P(("dp", "seq"), "mp"),
        P(("dp", "seq"), "mp"),
        P(("dp", "seq"), "mp"),
        P(("dp", "seq"), "mp"),
        P(),
        P(),
        P(),
        P(("dp", "seq"), "mp"),
        P(("dp", "seq"), "mp"),
        P(("dp", "seq"), "mp"),
        P("dp", "seq", None),
    )
    out_specs = (
        P("dp", "seq", None),
        P("dp", "seq", None),
        P(),
        P(("dp", "seq"), "mp"),
        P(("dp", "seq"), "mp"),
        P(("dp", "seq"), "mp"),
        P(("dp", "seq"), "mp"),
        P(),
        P(),
        P(),
        P(("dp", "seq"), "mp"),
        P(("dp", "seq"), "mp"),
        P(("dp", "seq"), "mp"),
    )
    return jax.shard_map(
        per_device, mesh=mesh, in_specs=in_specs, out_specs=out_specs, check_vma=False
    )
```

profile of v0, /device:TPU:0, one launch (start us, length us, event | category | flops | bytes accessed | tf_op | source)
XLA Modules:
  0.0 1509.3 jit_solution(13400549713124726164)
XLA Ops:
  12.8 42.5 %all-gather.12.cloned.1.call-done = bf16[1536,768]{1,0:T(8,128)(2,1)} async-done(((bf16[96,768]{1,0:T(8,128)(2,1)}), bf16[1536,768]{1,0:T(8,128)(2,1)}) %all-gather.12.cloned.1.call-update) | async-done | bytes 2359312 | tf_op jit(solution)/shard_map/all_gather | solution.py:165
  59.6 39.1 %all-gather.10.cloned.1.call-done = bf16[1536,768]{1,0:T(8,128)(2,1)} async-done(((bf16[96,768]{1,0:T(8,128)(2,1)}), bf16[1536,768]{1,0:T(8,128)(2,1)}) %all-gather.10.cloned.1.call-update) | async-done | bytes 2359312 | tf_op jit(solution)/shard_map/all_gather | solution.py:164
  107.8 34.2 %all-gather.16.cloned.1.call-done = bf16[1536,768]{1,0:T(8,128)(2,1)} async-done(((bf16[96,768]{1,0:T(8,128)(2,1)}), bf16[1536,768]{1,0:T(8,128)(2,1)}) %all-gather.16.cloned.1.call-update) | async-done | bytes 2359312 | tf_op jit(solution)/shard_map/all_gather | solution.py:166
  151.3 11.3 all-gather.14.cloned.1.call-done
  166.7 17.5 %all-gather.18.cloned.1.call-done = bf16[1024,768]{1,0:T(8,128)(2,1)} async-done(((bf16[256,768]{1,0:T(8,128)(2,1)}), bf16[1024,768]{1,0:T(8,128)(2,1)}) %all-gather.18.cloned.1.call-update) | async-done | bytes 1572880 | tf_op jit(solution)/shard_map/all_gather | solution.py:204
  187.6 45.8 %while.30 = (s32[]{:T(128)}, f32[6,256,128]{1,2,0:T(8,128)S(1)}, f32[6,256,128]{1,2,0:T(8,128)}, f32[6,2,256]{2,1,0:T(2,128)}, bf16[6,2,256,64]{3,2,1,0:T(8,128)...) while((s32[]{:T(128)}, f32[6,256,128]{1,2,0:T(8,128)S(1)}, ...), condition=%wide.region_9.10_spmd.clone, body=%wide.region_4.9_spmd.clone.sunk | while | flops 207093760 | bytes 7771785 | solution.py:211
  242.6 48.8 %all-reduce.6.cloned.1.call-done = f32[256,1536]{1,0:T(8,128)} async-done(((f32[256,1536]{1,0:T(8,128)}), f32[256,1536]{1,0:T(8,128)}) %all-reduce.6.cloned.1.call-update) | async-done | bytes 1572880 | tf_op jit(solution)/shard_map/psum | solution.py:226
  294.8 60.3 %all-gather.22.cloned.1.call-done = bf16[1536,2048]{1,0:T(8,128)(2,1)} async-done(((bf16[96,2048]{1,0:T(8,128)(2,1)}), bf16[1536,2048]{1,0:T(8,128)(2,1)}) %all-gather.22.cloned.1.call-update) | async-done | bytes 6291472 | tf_op jit(solution)/shard_map/all_gather | solution.py:168
  361.3 56.3 %all-gather.24.cloned.1.call-done = bf16[1536,2048]{1,0:T(8,128)(2,1)} async-done(((bf16[96,2048]{1,0:T(8,128)(2,1)}), bf16[1536,2048]{1,0:T(8,128)(2,1)}) %all-gather.24.cloned.1.call-update) | async-done | bytes 6291472 | tf_op jit(solution)/shard_map/all_gather | solution.py:169
  423.7 56.1 %all-gather.26.cloned.1.call-done = bf16[1536,2048]{1,0:T(8,128)(2,1)} async-done(((bf16[96,2048]{1,0:T(8,128)(2,1)}), bf16[1536,2048]{1,0:T(8,128)(2,1)}) %all-gather.26.cloned.1.call-update) | async-done | bytes 6291472 | tf_op jit(solution)/shard_map/all_gather | solution.py:170
  479.8 7.6 multiply_convert_fusion.2
  497.5 50.1 %all-reduce.8.cloned.1.call-done = f32[256,1536]{1,0:T(8,128)} async-done(((f32[256,1536]{1,0:T(8,128)}), f32[256,1536]{1,0:T(8,128)}) %all-reduce.8.cloned.1.call-update) | async-done | bytes 1572880 | tf_op jit(solution)/shard_map/psum | solution.py:250
  554.3 97.9 %while.31 = (s32[]{:T(128)}, f32[6,2,256,64]{2,3,1,0:T(8,128)}, bf16[6,2,1024,64]{2,3,1,0:T(8,128)(2,1)}, bf16[6,1024,128]{1,2,0:T(8,128)(2,1)}, bf16[6,2,256,64...) while((s32[]{:T(128)}, f32[6,2,256,64]{2,3,1,0:T(8,128)}, ...), condition=%wide.region_22.23_spmd.clone, body=%wide.region_19.22_spmd.clone.sunk | while | flops 477396480 | bytes 21397168 | solution.py:266
  658.8 21.5 %reduce-scatter.10.cloned.1.call-done = bf16[256,768]{0,1:T(8,128)(2,1)} async-done(((bf16[1024,768]{0,1:T(8,128)(2,1)}), bf16[256,768]{0,1:T(8,128)(2,1)}) %reduce-scatter.10.cloned.1.call-update) | async-done | bytes 393232 | tf_op jit(solution)/shard_map/reduce_scatter | solution.py:285
  687.1 23.8 %reduce-scatter.12.cloned.1.call-done = bf16[256,768]{0,1:T(8,128)(2,1)} async-done(((bf16[1024,768]{0,1:T(8,128)(2,1)}), bf16[256,768]{0,1:T(8,128)(2,1)}) %reduce-scatter.12.cloned.1.call-update) | async-done | bytes 393232 | tf_op jit(solution)/shard_map/reduce_scatter | solution.py:288
  749.6 6.5 fusion.84
  756.9 40.0 %all-reduce = (f32[1536]{0:T(1024)}, f32[128]{0:T(128)}, f32[]{:T(128)}, f32[1536]{0:T(1024)}) all-reduce(f32[1536]{0:T(1024)S(1)} %copy-done.37, f32[128]{0:T(128)S(1)} %broadcast_multiply_fusion.3, f32[]{:T(128)S(6)} %neg.15, f32[1536]{0:T(1024)S(1)} %copy-done.36), channel_id=1, replica_groups=mesh['dp'=4,'seq'=4,'mp'=2] {'dp','seq','mp'}, use_global_device_ids=true, to_apply=%region_28.29 | all-reduce | flops 3201 | bytes 25608 | tf_op jit(solution)/shard_map/psum | solution.py:311
  802.3 46.2 %reduce-scatter.20.cloned.1.call-done = f32[96,768]{1,0:T(8,128)} async-done(((f32[1536,768]{1,0:T(8,128)}), f32[96,768]{1,0:T(8,128)}) %reduce-scatter.20.cloned.1.call-update) | async-done | bytes 294928 | tf_op jit(solution)/shard_map/reduce_scatter | solution.py:327
  848.5 79.1 %reduce-scatter.14.cloned.1.call-done = f32[96,768]{1,0:T(8,128)} async-done(((f32[1536,768]{1,0:T(8,128)}), f32[96,768]{1,0:T(8,128)}) %reduce-scatter.14.cloned.1.call-update) | async-done | bytes 294928 | tf_op jit(solution)/shard_map/reduce_scatter | solution.py:324
  927.6 79.1 %reduce-scatter.16.cloned.1.call-done = f32[96,768]{1,0:T(8,128)} async-done(((f32[1536,768]{1,0:T(8,128)}), f32[96,768]{1,0:T(8,128)}) %reduce-scatter.16.cloned.1.call-update) | async-done | bytes 294928 | tf_op jit(solution)/shard_map/reduce_scatter | solution.py:325
  1006.7 79.1 %reduce-scatter.18.cloned.1.call-done = f32[96,768]{1,0:T(8,128)} async-done(((f32[1536,768]{1,0:T(8,128)}), f32[96,768]{1,0:T(8,128)}) %reduce-scatter.18.cloned.1.call-update) | async-done | bytes 294928 | tf_op jit(solution)/shard_map/reduce_scatter | solution.py:326
  1085.8 138.7 %reduce-scatter.22.cloned.1.call-done = f32[96,2048]{1,0:T(8,128)} async-done(((f32[1536,2048]{1,0:T(8,128)}), f32[96,2048]{1,0:T(8,128)}) %reduce-scatter.22.cloned.1.call-update) | async-done | bytes 786448 | tf_op jit(solution)/shard_map/reduce_scatter | solution.py:328
  1224.5 138.7 %reduce-scatter.24.cloned.1.call-done = f32[96,2048]{1,0:T(8,128)} async-done(((f32[1536,2048]{1,0:T(8,128)}), f32[96,2048]{1,0:T(8,128)}) %reduce-scatter.24.cloned.1.call-update) | async-done | bytes 786448 | tf_op jit(solution)/shard_map/reduce_scatter | solution.py:329
  1363.2 138.9 %reduce-scatter.26.cloned.1.call-done = f32[96,2048]{1,0:T(8,128)} async-done(((f32[1536,2048]{1,0:T(8,128)}), f32[96,2048]{1,0:T(8,128)}) %reduce-scatter.26.cloned.1.call-update) | async-done | bytes 786448 | tf_op jit(solution)/shard_map/reduce_scatter | solution.py:330
  (378 shorter events, 274.7 us)
Async XLA Ops:
  7.2 48.2 %all-gather.12.cloned.1.call-start = ((), (), s32[]{:S(2)}) async-start(), calls=%async_computation.10 | async-start | bytes 2506752 | tf_op jit(solution)/shard_map/all_gather | solution.py:165
  7.9 90.8 %all-gather.10.cloned.1.call-start = ((), (), s32[]{:S(2)}) async-start(), calls=%async_computation.9 | async-start | bytes 2506752 | tf_op jit(solution)/shard_map/all_gather | solution.py:164
  8.7 133.4 %all-gather.16.cloned.1.call-start = ((), (), s32[]{:S(2)}) async-start(), calls=%async_computation.12 | async-start | bytes 2506752 | tf_op jit(solution)/shard_map/all_gather | solution.py:166
  9.4 153.2 %all-gather.14.cloned.1.call-start = ((), (), s32[]{:S(2)}) async-start(), calls=%async_computation.11 | async-start | bytes 1966080 | tf_op jit(solution)/shard_map/all_gather | solution.py:203
  12.6 129.4 %copy-start.29 = (f32[256]{0:T(256)}, f32[256]{0:T(256)S(1)}, u32[]{:S(2)}) copy-start(f32[256]{0:T(256)S(1)} %add_rsqrt_fusion.2) | copy-start | bytes 3076
  12.8 93.9 %copy-start.25 = (f32[256,32]{0,1:T(8,128)}, f32[256,32]{0,1:T(8,128)S(1)}, u32[]{:S(2)}) copy-start(f32[256,32]{0,1:T(8,128)S(1)} %get-tuple-element.310) | copy-start | bytes 98308
  12.8 93.9 %copy-start.27 = (f32[256,32]{0,1:T(8,128)}, f32[256,32]{0,1:T(8,128)S(1)}, u32[]{:S(2)}) copy-start(f32[256,32]{0,1:T(8,128)S(1)} %get-tuple-element.311) | copy-start | bytes 98308
  107.7 76.5 %all-gather.18.cloned.1.call-start = ((), (), s32[]{:S(2)}) async-start(), calls=%async_computation.13 | async-start | bytes 1966080 | tf_op jit(solution)/shard_map/all_gather | solution.py:204
  145.3 90.6 %all-gather.20.cloned.1.call-start = ((), (), s32[]{:S(2)}) async-start(), calls=%async_computation.14 | async-start | bytes 2506752 | tf_op jit(solution)/shard_map/all_gather | solution.py:167
  145.9 145.5 %all-reduce.6.cloned.1.call-start = ((), (), s32[]{:S(2)}) async-start(), calls=%async_computation.15 | async-start | bytes 3145728 | tf_op jit(solution)/shard_map/psum | solution.py:226
  239.6 115.5 %all-gather.22.cloned.1.call-start = ((), (), s32[]{:S(2)}) async-start(), calls=%async_computation.16 | async-start | bytes 6684672 | tf_op jit(solution)/shard_map/all_gather | solution.py:168
  240.4 177.2 %all-gather.24.cloned.1.call-start = ((), (), s32[]{:S(2)}) async-start(), calls=%async_computation.17 | async-start | bytes 6684672 | tf_op jit(solution)/shard_map/all_gather | solution.py:169
  241.1 238.7 %all-gather.26.cloned.1.call-start = ((), (), s32[]{:S(2)}) async-start(), calls=%async_computation.18 | async-start | bytes 6684672 | tf_op jit(solution)/shard_map/all_gather | solution.py:170
  241.7 305.9 %all-reduce.8.cloned.1.call-start = ((), (), s32[]{:S(2)}) async-start(), calls=%async_computation.19 | async-start | bytes 3145728 | tf_op jit(solution)/shard_map/psum | solution.py:250
  497.2 183.2 %reduce-scatter.10.cloned.1.call-start = ((), (), s32[]{:S(2)}) async-start(), calls=%async_computation.20 | async-start | bytes 1966080 | tf_op jit(solution)/shard_map/reduce_scatter | solution.py:285
  652.2 58.8 %reduce-scatter.12.cloned.1.call-start = ((), (), s32[]{:S(2)}) async-start(), calls=%async_computation.21 | async-start | bytes 1966080 | tf_op jit(solution)/shard_map/reduce_scatter | solution.py:288
  652.9 145.8 %all-reduce.10.cloned.1.call-start = ((), (), s32[]{:S(2)}) async-start(), calls=%async_computation.29 | async-start | bytes 3145728 | tf_op jit(solution)/shard_map/psum | solution.py:236
  716.3 132.2 %reduce-scatter.20.cloned.1.call-start = ((), (), s32[]{:S(2)}) async-start(), calls=%async_computation.25 | async-start | bytes 5013504 | tf_op jit(solution)/shard_map/reduce_scatter | solution.py:327
  720.4 207.2 %reduce-scatter.14.cloned.1.call-start = ((), (), s32[]{:S(2)}) async-start(), calls=%async_computation.22 | async-start | bytes 5013504 | tf_op jit(solution)/shard_map/reduce_scatter | solution.py:324
  724.4 282.2 %reduce-scatter.16.cloned.1.call-start = ((), (), s32[]{:S(2)}) async-start(), calls=%async_computation.23 | async-start | bytes 5013504 | tf_op jit(solution)/shard_map/reduce_scatter | solution.py:325
  728.6 357.2 %reduce-scatter.18.cloned.1.call-start = ((), (), s32[]{:S(2)}) async-start(), calls=%async_computation.24 | async-start | bytes 5013504 | tf_op jit(solution)/shard_map/reduce_scatter | solution.py:326
  732.6 491.9 %reduce-scatter.22.cloned.1.call-start = ((), (), s32[]{:S(2)}) async-start(), calls=%async_computation.26 | async-start | bytes 13369344 | tf_op jit(solution)/shard_map/reduce_scatter | solution.py:328
  740.5 622.7 %reduce-scatter.24.cloned.1.call-start = ((), (), s32[]{:S(2)}) async-start(), calls=%async_computation.27 | async-start | bytes 13369344 | tf_op jit(solution)/shard_map/reduce_scatter | solution.py:329
  748.0 754.0 %reduce-scatter.26.cloned.1.call-start = ((), (), s32[]{:S(2)}) async-start(), calls=%async_computation.28 | async-start | bytes 13369344 | tf_op jit(solution)/shard_map/reduce_scatter | solution.py:330
  (48 other events, 292.1 us)
Sparse Core Ops, SparseCore 0:
  10.3 45.0 all-gather.11
  57.6 41.0 all-gather.9
  101.0 41.0 all-gather.15
  144.0 18.5 all-gather.13
  164.6 19.6 all-gather.17
  186.4 42.3 all-gather.19
  239.7 51.6 all-reduce.5
  293.7 61.3 all-gather.21
  357.4 60.0 all-gather.23
  419.7 60.0 all-gather.25
  497.3 50.2 all-reduce.7
  652.3 28.0 reduce-scatter.9
  682.9 27.9 reduce-scatter.11
  716.4 52.0 all-reduce.9
  772.8 75.6 reduce-scatter.19
  852.8 74.7 reduce-scatter.13
  931.9 74.7 reduce-scatter.15
  1011.0 74.7 reduce-scatter.17
  1090.4 134.0 reduce-scatter.21
  1229.0 134.1 reduce-scatter.23
  1367.8 134.1 reduce-scatter.25
where the time goes:
time: 1520 us; the launch traced here: 1510 us
  waiting for transfers between devices  1170 us (77%)
  matrix products  199 us (13%)
  other arithmetic  44.6 us (3%)
  blocking collectives  40 us (3%)
  local copies, waits for them, and re-layouts  38.5 us (3%)
  between operations  18.7 us (1%)
    reduce_scatter x1, waiting for transfers between devices, per_device(): lax.psum_scatter(down_grad, ('dp', 'seq'), scatter_dimension=0, tiled=True)  139 us
    reduce_scatter x1, waiting for transfers between devices, per_device(): lax.psum_scatter(gate_grad, ('dp', 'seq'), scatter_dimension=0, tiled=True)  139 us
    reduce_scatter x1, waiting for transfers between devices, per_device(): lax.psum_scatter(up_grad, ('dp', 'seq'), scatter_dimension=0, tiled=True)  139 us
    reduce_scatter x1, waiting for transfers between devices, per_device(): lax.psum_scatter(value_weight_grad, ('dp', 'seq'), scatter_dimension=0, t...  79.1 us
    reduce_scatter x1, waiting for transfers between devices, per_device(): lax.psum_scatter(query_grad, ('dp', 'seq'), scatter_dimension=0, tiled=True)  79.1 us
    reduce_scatter x1, waiting for transfers between devices, per_device(): lax.psum_scatter(key_grad, ('dp', 'seq'), scatter_dimension=0, tiled=True)  79.1 us
    all_gather x1, waiting for transfers between devices, per_device(): lax.all_gather(gate_weight, ('dp', 'seq'), axis=0, tiled=True)  60.3 us
    all_gather x1, waiting for transfers between devices, per_device(): lax.all_gather(up_weight, ('dp', 'seq'), axis=0, tiled=True)  56.3 us
  transfers between devices with their start and end apart: 21, of which 19 were waited for; matrix products, arithmetic and copies ran while one was open for 9% of the time, Pallas kernels for 0%

commit v1 on v0

v1 whole, which is shorter than its diff:
```python
import functools
import math

import jax
import jax.numpy as jnp
from jax import lax
from jax.experimental import pallas as pl
from jax.experimental.pallas import tpu as pltpu
from jax.sharding import PartitionSpec as P

EPSILON = 1e-05
LAMBDA_INIT = 0.2
OUTPUT_SCALE = 1.0 - LAMBDA_INIT
NEGATIVE = -1e30
MOST_DOC = 512
F32 = jnp.float32
BF16 = jnp.bfloat16


def dot(a, b):
    return lax.dot_general(a, b, (((1,), (0,)), ((), ())), preferred_element_type=F32)


def dot_nt(a, b):
    return lax.dot_general(a, b, (((1,), (1,)), ((), ())), preferred_element_type=F32)


def dot_tn(a, b):
    return lax.dot_general(a, b, (((0,), (0,)), ((), ())), preferred_element_type=F32)


def full_spec(shape):
    return pl.BlockSpec(shape, lambda *_: (0,) * len(shape))


def cost(flops, moved, special=0):
    return pl.CostEstimate(flops=int(flops), bytes_accessed=int(moved), transcendentals=int(special))


def swap_halves(values, quarter):
    width = 4 * quarter
    lane = lax.broadcasted_iota(jnp.int32, values.shape, 1)
    ahead = pltpu.roll(values, width - quarter, 1)
    behind = pltpu.roll(values, quarter, 1)
    return jnp.where((lane % (2 * quarter)) < quarter, ahead, behind)


def qkv_kernel(rotated, head_width, x_ref, gain_ref, cos_ref, sin_ref, w_ref, out_ref, normed_ref):
    step = pl.program_id(0)

    @pl.when(step == 0)
    def _():
        values = x_ref[...].astype(F32)
        inverse = lax.rsqrt(jnp.mean(values * values, axis=-1, keepdims=True) + EPSILON)
        normed_ref[...] = (values * inverse * gain_ref[...]).astype(BF16)

    product = dot(normed_ref[...], w_ref[...])

    @pl.when(step < rotated)
    def _():
        for start in range(0, product.shape[1], head_width):
            piece = product[:, start : start + head_width]
            turned = piece * cos_ref[...] + swap_halves(piece, head_width // 4) * sin_ref[...]
            out_ref[:, start : start + head_width] = turned.astype(BF16)

    @pl.when(step >= rotated)
    def _():
        out_ref[...] = product.astype(BF16)


def project_qkv(x, gain, cos_table, sin_table, weights, width, head_width):
    length, model = x.shape
    tile = 256
    return pl.pallas_call(
        functools.partial(qkv_kernel, 2 * width // tile, head_width),
        grid=(3 * width // tile,),
        in_specs=[
            full_spec((length, model)),
            full_spec((1, model)),
            full_spec((length, head_width)),
            full_spec((length, head_width)),
            pl.BlockSpec((model, tile), lambda j: (0, j)),
        ],
        out_specs=[
            pl.BlockSpec((length, tile), lambda j: (0, j)),
            full_spec((length, model)),
        ],
        out_shape=[
            jax.ShapeDtypeStruct((length, 3 * width), BF16),
            jax.ShapeDtypeStruct((length, model), BF16),
        ],
        cost_estimate=cost(6 * length * model * width, 6 * model * width + 8 * length * width),
        name="qkv_project",
    )(x, gain, cos_table, sin_table, weights)


def masks_of(seg_q, seg_k_ref, blocks):
    length = seg_q.shape[0]
    allowed = []
    for b in range(blocks):
        same = seg_q == seg_k_ref[b : b + 1, :]
        if b == 0:
            rows = lax.broadcasted_iota(jnp.int32, (length, length), 0)
            columns = lax.broadcasted_iota(jnp.int32, (length, length), 1)
            same = same & (rows >= columns)
        allowed.append(same)
    return allowed


def attend_kernel(blocks, *refs):
    lam_ref, seg_q_ref, seg_k_ref, gain_ref, q_ref = refs[:5]
    k_refs = refs[5 : 5 + blocks]
    v_refs = refs[5 + blocks : 5 + 2 * blocks]
    normed_ref, mixture_ref, second_ref, logsum_ref = refs[5 + 2 * blocks :]
    half = q_ref.shape[1] // 2
    scale = half ** (-0.5)
    allowed = masks_of(seg_q_ref[...], seg_k_ref, blocks)
    outputs = []
    for j in range(2):
        cut = slice(j * half, (j + 1) * half)
        query = q_ref[:, cut]
        scores = [
            jnp.where(allowed[b], dot_nt(query, k_refs[b][:, cut]) * scale, NEGATIVE)
            for b in range(blocks)
        ]
        highest = functools.reduce(
            jnp.maximum, [jnp.max(s, axis=-1, keepdims=True) for s in scores]
        )
        exponents = [jnp.exp(s - highest) for s in scores]
        total = sum(jnp.sum(e, axis=-1, keepdims=True) for e in exponents)
        inverse = 1.0 / total
        outputs.append(
            sum(dot((exponents[b] * inverse).astype(BF16), v_refs[b][...]) for b in range(blocks))
        )
        logsum_ref[0, :, j : j + 1] = highest + jnp.log(total)
    mixture = outputs[0] - lam_ref[0, 0] * outputs[1]
    inverse_head = lax.rsqrt(jnp.mean(mixture * mixture, axis=-1, keepdims=True) + EPSILON)
    normed_ref[...] = (mixture * inverse_head * (gain_ref[...] * OUTPUT_SCALE)).astype(BF16)
    mixture_ref[...] = mixture
    second_ref[...] = outputs[1]


def attend(lam, seg_q, seg_k, head_gain, qkv, prior, heads, head_width):
    length = qkv.shape[0]
    blocks = seg_k.shape[0]
    block = (length, head_width)

    def at(first):
        return pl.BlockSpec(block, lambda h: (0, first + h))

    width = heads * head_width
    return pl.pallas_call(
        functools.partial(attend_kernel, blocks),
        grid=(heads,),
        in_specs=[
            pl.BlockSpec(memory_space=pltpu.SMEM),
            full_spec(seg_q.shape),
            full_spec(seg_k.shape),
            full_spec(head_gain.shape),
            at(0),
            at(heads),
            *[at(0) for _ in prior],
            at(2 * heads),
            *[at(heads) for _ in prior],
        ],
        out_specs=[at(0), at(0), at(0), pl.BlockSpec((1, length, 2), lambda h: (h, 0, 0))],
        out_shape=[
            jax.ShapeDtypeStruct((length, width), BF16),
            jax.ShapeDtypeStruct((length, width), F32),
            jax.ShapeDtypeStruct((length, width), F32),
            jax.ShapeDtypeStruct((heads, length, 2), F32),
        ],
        cost_estimate=cost(
            8 * heads * length * length * blocks * head_width,
            length * width * (2 + 4 * blocks + 10),
            2 * heads * length * length * blocks,
        ),
        name="attend_forward",
    )(lam, seg_q, seg_k, head_gain, qkv, qkv, *prior, qkv, *prior)


def feed_kernel(
    x_ref, own_ref, other_ref, gain_ref, cot_ref, usable_ref, gate_ref, up_ref, down_ref,
    hidden_ref, normed_ref, low_ref, inner_ref, grad_gate_ref, grad_up_ref,
    part_ref, back_ref, gain_part_ref, sum_out, sum_back, inverse_ref,
):
    step = pl.program_id(0)
    gain = gain_ref[...]

    @pl.when(step == 0)
    def _():
        hidden = x_ref[...].astype(F32) + (own_ref[...].astype(F32) + other_ref[...].astype(F32))
        inverse = lax.rsqrt(jnp.mean(hidden * hidden, axis=-1, keepdims=True) + EPSILON)
        hidden_ref[...] = hidden
        inverse_ref[...] = inverse
        normed_ref[...] = (hidden * inverse * gain).astype(BF16)
        low_ref[...] = (cot_ref[...].astype(F32) * usable_ref[...]).astype(BF16)
        sum_out[...] = jnp.zeros_like(sum_out)
        sum_back[...] = jnp.zeros_like(sum_back)

    normed = normed_ref[...]
    gate = dot(normed, gate_ref[...])
    up = dot(normed, up_ref[...])
    grad_inner = dot(low_ref[...], down_ref[...])
    sigmoid = jax.nn.sigmoid(gate)
    silu = gate * sigmoid
    inner = (silu * up).astype(BF16)
    grad_gate = (grad_inner * up * (sigmoid * (1.0 + gate * (1.0 - sigmoid)))).astype(BF16)
    grad_up = (grad_inner * silu).astype(BF16)
    inner_ref[...] = inner
    grad_gate_ref[...] = grad_gate
    grad_up_ref[...] = grad_up
    sum_out[...] += dot_nt(inner, down_ref[...])
    sum_back[...] += dot_nt(grad_gate, gate_ref[...]) + dot_nt(grad_up, up_ref[...])

    @pl.when(step == pl.num_programs(0) - 1)
    def _():
        part_ref[...] = sum_out[...].astype(BF16)
        inverse = inverse_ref[...]
        unit = hidden_ref[...] * inverse
        grad = sum_back[...]
        weighed = gain * grad
        gain_part_ref[...] = jnp.sum(grad * unit, axis=0, keepdims=True)
        centre = jnp.mean(weighed * unit, axis=-1, keepdims=True)
        back_ref[...] = (inverse * (weighed - unit * centre)).astype(BF16)


def feed_forward(x, own, other, gain, cotangent, usable, weights, hidden_units):
    length, model = x.shape
    tile = 256
    tiles = hidden_units // tile
    whole = (length, model)

    def weight_at(first):
        return pl.BlockSpec((model, tile), lambda j: (0, first * tiles + j))

    column = pl.BlockSpec((length, tile), lambda j: (0, j))
    return pl.pallas_call(
        feed_kernel,
        grid=(tiles,),
        in_specs=[
            full_spec(whole), full_spec(whole), full_spec(whole), full_spec((1, model)),
            full_spec(whole), full_spec((length, 1)), weight_at(0), weight_at(1), weight_at(2),
        ],
        out_specs=[
            full_spec(whole), full_spec(whole), full_spec(whole), column, column, column,
            full_spec(whole), full_spec(whole), full_spec((1, model)),
        ],
        out_shape=[
            jax.ShapeDtypeStruct(whole, F32),
            jax.ShapeDtypeStruct(whole, BF16),
            jax.ShapeDtypeStruct(whole, BF16),
            *[jax.ShapeDtypeStruct((length, hidden_units), BF16)] * 3,
            jax.ShapeDtypeStruct(whole, BF16),
            jax.ShapeDtypeStruct(whole, BF16),
            jax.ShapeDtypeStruct((1, model), F32),
        ],
        scratch_shapes=[
            pltpu.VMEM(whole, F32), pltpu.VMEM(whole, F32), pltpu.VMEM((length, 1), F32),
        ],
        cost_estimate=cost(
            12 * length * model * hidden_units, 6 * model * hidden_units + 20 * length * model
        ),
        name="feed_forward",
    )(x, own, other, gain, cotangent, usable, weights, weights, weights)


def attend_back_kernel(blocks, *refs):
    (lam_ref, seg_q_ref, seg_k_ref, gain_ref, cos_ref, sin_ref, low_ref, own_ref, other_ref,
     out_weight_ref, mixture_ref, second_ref, logsum_ref, q_ref) = refs[:14]
    k_refs = refs[14 : 14 + blocks]
    v_refs = refs[14 + blocks : 14 + 2 * blocks]
    grad_hidden_ref, hidden_low_ref, grad_q_ref, own_kv_ref = refs[14 + 2 * blocks : 18 + 2 * blocks]
    prior_kv_refs = refs[18 + 2 * blocks : 17 + 3 * blocks]
    gain_part_ref, lam_part_ref = refs[17 + 3 * blocks :]
    step = pl.program_id(0)

    @pl.when(step == 0)
    def _():
        grad_hidden = low_ref[...].astype(F32) + (
            own_ref[...].astype(F32) + other_ref[...].astype(F32)
        )
        grad_hidden_ref[...] = grad_hidden
        hidden_low_ref[...] = grad_hidden.astype(BF16)
        gain_part_ref[...] = jnp.zeros_like(gain_part_ref)
        lam_part_ref[...] = jnp.zeros_like(lam_part_ref)

    head_width = q_ref.shape[1]
    half = head_width // 2
    scale = half ** (-0.5)
    lam = lam_ref[0, 0]
    grad_head = dot(hidden_low_ref[...], out_weight_ref[...])
    mixture = mixture_ref[...]
    inverse_head = lax.rsqrt(jnp.mean(mixture * mixture, axis=-1, keepdims=True) + EPSILON)
    unit_head = mixture * inverse_head
    gain_part_ref[...] += jnp.sum(grad_head * unit_head, axis=0, keepdims=True) * OUTPUT_SCALE
    weighed = gain_ref[...] * OUTPUT_SCALE * grad_head
    centre_head = jnp.mean(weighed * unit_head, axis=-1, keepdims=True)
    grad_mixture = inverse_head * (weighed - unit_head * centre_head)
    lam_part_ref[...] -= jnp.sum(grad_mixture * second_ref[...], axis=0, keepdims=True)
    grads = (grad_mixture.astype(BF16), (-lam * grad_mixture).astype(BF16))
    allowed = masks_of(seg_q_ref[...], seg_k_ref, blocks)
    grad_queries = []
    grad_keys = [[] for _ in range(blocks)]
    grad_values = [0.0] * blocks
    for j in range(2):
        cut = slice(j * half, (j + 1) * half)
        query = q_ref[:, cut]
        grad_out = grads[j]
        logsum = logsum_ref[0, :, j : j + 1]
        soft, grad_soft = [], []
        for b in range(blocks):
            scores = dot_nt(query, k_refs[b][:, cut]) * scale
            soft.append(jnp.exp(jnp.where(allowed[b], scores - logsum, NEGATIVE)))
            grad_soft.append(dot_nt(grad_out, v_refs[b][...]))
            grad_values[b] = grad_values[b] + dot_tn(soft[b].astype(BF16), grad_out)
        centre = sum(jnp.sum(soft[b] * grad_soft[b], axis=-1, keepdims=True) for b in range(blocks))
        grad_query = 0.0
        for b in range(blocks):
            grad_scores = (scale * soft[b] * (grad_soft[b] - centre)).astype(BF16)
            grad_query = grad_query + dot(grad_scores, k_refs[b][:, cut])
            grad_keys[b].append(dot_tn(grad_scores, query))
        grad_queries.append(grad_query)
    grad_query = jnp.concatenate(grad_queries, axis=1)
    turned = grad_query * cos_ref[...] - swap_halves(grad_query, head_width // 4) * sin_ref[...]
    grad_q_ref[...] = turned.astype(BF16)
    for b, ref in enumerate((own_kv_ref, *prior_kv_refs)):
        ref[:, :head_width] = jnp.concatenate(grad_keys[b], axis=1).astype(ref.dtype)
        ref[:, head_width:] = grad_values[b].astype(ref.dtype)


def attend_back(
    lam, seg_q, seg_k, head_gain, cos_table, sin_table, grad_low, own, other, weights,
    mixture, second, logsum, qkv, prior, heads, head_width,
):
    length, model = grad_low.shape
    blocks = seg_k.shape[0]
    whole = (length, model)
    width = heads * head_width

    def at(first):
        return pl.BlockSpec((length, head_width), lambda h: (0, first + h))

    pair = pl.BlockSpec((length, 2 * head_width), lambda h: (0, h))
    return pl.pallas_call(
        functools.partial(attend_back_kernel, blocks),
        grid=(heads,),
        in_specs=[
            pl.BlockSpec(memory_space=pltpu.SMEM),
            full_spec(seg_q.shape), full_spec(seg_k.shape), full_spec(head_gain.shape),
            full_spec((length, head_width)), full_spec((length, head_width)),
            full_spec(whole), full_spec(whole), full_spec(whole),
            pl.BlockSpec((model, head_width), lambda h: (0, 3 * heads + h)),
            at(0), at(0), pl.BlockSpec((1, length, 2), lambda h: (h, 0, 0)),
            at(0),
            at(heads), *[at(0) for _ in prior],
            at(2 * heads), *[at(heads) for _ in prior],
        ],
        out_specs=[
            full_spec(whole), full_spec(whole), at(0), pair, *[pair for _ in prior],
            full_spec((1, head_width)), full_spec((1, head_width)),
        ],
        out_shape=[
            jax.ShapeDtypeStruct(whole, F32),
            jax.ShapeDtypeStruct(whole, BF16),
            jax.ShapeDtypeStruct((length, width), BF16),
            jax.ShapeDtypeStruct((length, 2 * width), F32),
            *[jax.ShapeDtypeStruct((length, 2 * width), BF16) for _ in prior],
            jax.ShapeDtypeStruct((1, head_width), F32),
            jax.ShapeDtypeStruct((1, head_width), F32),
        ],
        cost_estimate=cost(
            24 * heads * length * length * blocks * head_width + 2 * length * model * width,
            2 * model * width + 24 * length * model,
            2 * heads * length * length * blocks,
        ),
        name="attend_backward",
    )(
        lam, seg_q, seg_k, head_gain, cos_table, sin_table, grad_low, own, other, weights,
        mixture, second, logsum, qkv, qkv, *prior, qkv, *prior,
    )


def input_back_kernel(
    arrivals, *refs,
):
    x_ref, gain_ref, cos_ref, sin_ref, grad_q_ref, own_ref = refs[:6]
    arrival_refs = refs[6 : 6 + arrivals]
    wq_ref, wk_ref, wv_ref, grad_k_ref, grad_v_ref, back_ref, gain_part_ref, total = refs[6 + arrivals :]
    step = pl.program_id(0)
    head_width = grad_q_ref.shape[1]
    pair = own_ref[...]
    for ref in arrival_refs:
        pair = pair + ref[...].astype(F32)
    grad_key = pair[:, :head_width]
    turned = grad_key * cos_ref[...] - swap_halves(grad_key, head_width // 4) * sin_ref[...]
    grad_k = turned.astype(BF16)
    grad_v = pair[:, head_width:].astype(BF16)
    grad_k_ref[...] = grad_k
    grad_v_ref[...] = grad_v

    @pl.when(step == 0)
    def _():
        total[...] = jnp.zeros_like(total)

    total[...] += (
        dot_nt(grad_q_ref[...], wq_ref[...])
        + dot_nt(grad_k, wk_ref[...])
        + dot_nt(grad_v, wv_ref[...])
    )

    @pl.when(step == pl.num_programs(0) - 1)
    def _():
        values = x_ref[...].astype(F32)
        inverse = lax.rsqrt(jnp.mean(values * values, axis=-1, keepdims=True) + EPSILON)
        unit = values * inverse
        grad = total[...]
        weighed = gain_ref[...] * grad
        gain_part_ref[...] = jnp.sum(grad * unit, axis=0, keepdims=True)
        centre = jnp.mean(weighed * unit, axis=-1, keepdims=True)
        back_ref[...] = (inverse * (weighed - unit * centre)).astype(BF16)


def input_back(x, gain, cos_table, sin_table, grad_q, own, arrived, weights, heads, head_width):
    length, model = x.shape
    width = heads * head_width
    whole = (length, model)

    def weight_at(first):
        return pl.BlockSpec((model, head_width), lambda h: (0, first * heads + h))

    column = pl.BlockSpec((length, head_width), lambda h: (0, h))
    pair = pl.BlockSpec((length, 2 * head_width), lambda h: (0, h))
    return pl.pallas_call(
        functools.partial(input_back_kernel, len(arrived)),
        grid=(heads,),
        in_specs=[
            full_spec(whole), full_spec((1, model)),
            full_spec((length, head_width)), full_spec((length, head_width)),
            column, pair, *[pair for _ in arrived],
            weight_at(0), weight_at(1), weight_at(2),
        ],
        out_specs=[column, column, full_spec(whole), full_spec((1, model))],
        out_shape=[
            jax.ShapeDtypeStruct((length, width), BF16),
            jax.ShapeDtypeStruct((length, width), BF16),
            jax.ShapeDtypeStruct(whole, BF16),
            jax.ShapeDtypeStruct((1, model), F32),
        ],
        scratch_shapes=[pltpu.VMEM(whole, F32)],
        cost_estimate=cost(6 * length * model * width, 6 * model * width + 16 * length * model),
        name="input_backward",
    )(x, gain, cos_table, sin_table, grad_q, own, *arrived, weights, weights, weights)


def tables(doc_lengths, length):
    doc_count = doc_lengths.shape[0]
    doc_ends = jnp.cumsum(doc_lengths)
    places = jnp.arange(length, dtype=jnp.int32)
    segment = jnp.sum((places[:, None] >= doc_ends[None, :]).astype(jnp.int32), axis=1)
    matched = segment[:, None] == jnp.arange(doc_count, dtype=jnp.int32)[None, :]
    doc_start = jnp.sum(jnp.where(matched, (doc_ends - doc_lengths)[None, :], 0), axis=1)
    return (segment, places - doc_start, segment < doc_count - 1)


def rotary(position, half_width):
    pair_count = half_width // 2
    frequency = jnp.exp(
        jnp.arange(pair_count, dtype=F32) * (-2.0 * math.log(10000.0) / half_width)
    )
    angles = position.astype(F32)[:, None] * frequency[None, :]
    cosine, sine = jnp.cos(angles), jnp.sin(angles)
    return (
        jnp.concatenate([cosine] * 4, axis=1),
        jnp.concatenate([-sine, sine, -sine, sine], axis=1),
    )


def other_half(part):
    count = lax.axis_size("mp")
    return lax.ppermute(part, "mp", [(i, (i + 1) % count) for i in range(count)])


def shift(values, step):
    count = lax.axis_size("seq")
    pairs = [(i, i + step) for i in range(count) if 0 <= i + step < count]
    return lax.ppermute(values, "seq", pairs)


def weight_grad(left, right):
    return dot_tn(left, right).astype(BF16)


def per_device(
    tokens, doc_lengths, attention_gain, query_weight, key_weight, value_weight, output_weight,
    head_gain, lambda_vectors, feedforward_gain, gate_weight, up_weight, down_weight, cotangent,
):
    local_len = tokens.shape[1]
    seq_count = lax.axis_size("seq")
    row_len = local_len * seq_count
    me = lax.axis_index("seq")
    offset = me * local_len
    half_width = lambda_vectors.shape[1]
    head_width = 2 * half_width
    width = query_weight.shape[1]
    heads = width // head_width
    hidden_units = gate_weight.shape[1]
    back_steps = min(seq_count - 1, -(-(MOST_DOC - 1) // local_len))
    whole = ("dp", "seq")

    attention_weights = lax.all_gather(
        jnp.concatenate([query_weight, key_weight, value_weight, output_weight], axis=1),
        whole, axis=0, tiled=True,
    )
    feed_weights = lax.all_gather(
        jnp.concatenate([gate_weight, up_weight, down_weight], axis=1), whole, axis=0, tiled=True
    )

    segment, position, usable = tables(doc_lengths[0], row_len)
    local_segment = lax.dynamic_slice_in_dim(segment, offset, local_len)
    local_position = lax.dynamic_slice_in_dim(position, offset, local_len)
    local_usable = lax.dynamic_slice_in_dim(usable, offset, local_len).astype(F32)[:, None]
    by_block = segment.reshape(seq_count, local_len)
    key_segments = []
    for b in range(back_steps + 1):
        rows = lax.dynamic_index_in_dim(by_block, jnp.maximum(me - b, 0), 0, keepdims=True)
        key_segments.append(jnp.where(me >= b, rows, -1))
    seg_k = jnp.concatenate(key_segments, axis=0)
    seg_q = local_segment[:, None]
    cos_table, sin_table = rotary(local_position, half_width)
    first_exp = jnp.exp(jnp.sum(lambda_vectors[0] * lambda_vectors[1]))
    second_exp = jnp.exp(jnp.sum(lambda_vectors[2] * lambda_vectors[3]))
    lam = (first_exp - second_exp + LAMBDA_INIT).reshape(1, 1)
    gain_one = attention_gain[None]
    gain_two = feedforward_gain[None]
    gain_head = head_gain[None]
    inputs = tokens[0]

    qkv, normed_one = project_qkv(
        inputs, gain_one, cos_table, sin_table, attention_weights, width, head_width
    )
    prior = [shift(qkv[:, width:], b) for b in range(1, back_steps + 1)]
    normed_head, mixture, second, logsum = attend(
        lam, seg_q, seg_k, gain_head, qkv, prior, heads, head_width
    )
    attention_part = lax.optimization_barrier(
        dot_nt(normed_head, attention_weights[:, 3 * width :]).astype(BF16)
    )
    (
        hidden, normed_two, grad_low, inner, grad_gate, grad_up, feed_part, feed_back,
        feed_gain_part,
    ) = feed_forward(
        inputs, attention_part, other_half(attention_part), gain_two, cotangent[0], local_usable,
        feed_weights, hidden_units,
    )
    outs = attend_back(
        lam, seg_q, seg_k, gain_head, cos_table, sin_table, grad_low, feed_back,
        other_half(feed_back), attention_weights, mixture, second, logsum, qkv, prior, heads,
        head_width,
    )
    grad_hidden, hidden_low, grad_q, own_kv = outs[:4]
    prior_kv = outs[4 : 4 + back_steps]
    head_gain_part, lambda_part = outs[4 + back_steps :]
    result = hidden + (feed_part.astype(F32) + other_half(feed_part).astype(F32))
    feed_grads = lax.psum_scatter(
        jnp.concatenate(
            [
                weight_grad(normed_two, grad_gate),
                weight_grad(normed_two, grad_up),
                weight_grad(grad_low, inner),
            ],
            axis=1,
        ),
        whole, scatter_dimension=0, tiled=True,
    ).astype(F32)
    arrived = [shift(values, -(b + 1)) for b, values in enumerate(prior_kv)]
    grad_k, grad_v, input_part, attention_gain_part = input_back(
        inputs, gain_one, cos_table, sin_table, grad_q, own_kv, arrived, attention_weights, heads,
        head_width,
    )
    attention_grads = lax.psum_scatter(
        jnp.concatenate(
            [
                weight_grad(normed_one, grad_q),
                weight_grad(normed_one, grad_k),
                weight_grad(normed_one, grad_v),
                weight_grad(hidden_low, normed_head),
            ],
            axis=1,
        ),
        whole, scatter_dimension=0, tiled=True,
    ).astype(F32)
    grad_tokens = grad_hidden + (input_part.astype(F32) + other_half(input_part).astype(F32))
    gain_sums = lax.psum(
        jnp.concatenate(
            [
                attention_gain_part[0], feed_gain_part[0], head_gain_part[0],
                jnp.sum(lambda_part).reshape(1),
            ]
        ),
        ("dp", "seq", "mp"),
    )
    model = inputs.shape[1]
    lambda_total = gain_sums[-1]
    lambda_grad = jnp.stack(
        [
            lambda_total * first_exp * lambda_vectors[1],
            lambda_total * first_exp * lambda_vectors[0],
            -lambda_total * second_exp * lambda_vectors[3],
            -lambda_total * second_exp * lambda_vectors[2],
        ]
    )
    return (
        result.astype(BF16)[None],
        grad_tokens.astype(BF16)[None],
        gain_sums[:model],
        attention_grads[:, :width],
        attention_grads[:, width : 2 * width],
        attention_grads[:, 2 * width : 3 * width],
        attention_grads[:, 3 * width :],
        gain_sums[2 * model : 2 * model + head_width],
        lambda_grad,
        gain_sums[model : 2 * model],
        feed_grads[:, :hidden_units],
        feed_grads[:, hidden_units : 2 * hidden_units],
        feed_grads[:, 2 * hidden_units :],
    )


def solution(mesh):
    rows = P(("dp", "seq"), "mp")
    activations = P("dp", "seq", None)
    in_specs = (
        activations, P("dp", None), P(), rows, rows, rows, rows, P(), P(), P(), rows, rows, rows,
        activations,
    )
    out_specs = (
        activations, activations, P(), rows, rows, rows, rows, P(), P(), P(), rows, rows, rows,
    )
    return jax.shard_map(
        per_device, mesh=mesh, in_specs=in_specs, out_specs=out_specs, check_vma=False
    )
```

time: 1520 us -> 662 us (0.44)
  waiting for transfers between devices: 1170 us -> 435 us
  matrix products: 199 us -> 15.3 us
  Pallas kernels: 0 us -> 73.4 us
    reduce_scatter x9 -> x1, waiting for transfers between devices: 745 us -> 193 us  [per_device(): lax.psum_scatter(jnp.concatenate([weight_grad(normed_two, grad_gate), wei...]
    all_gather x9 -> x2, waiting for transfers between devices: 317 us -> 125 us  [the longest x1 80.2 us: per_device(): lax.all_gather(jnp.concatenate([query_weight, key_weight, value_weight, o...]
    dot_general x105 -> x8, matrix products: 199 us -> 15.3 us  [the longest x7 12.6 us: dot_tn(): lax.dot_general(a, b, (((0,), (0,)), ((), ())), preferred_element_type=F32)]
    ppermute x0 -> x8, waiting for transfers between devices: none -> 101 us  [the longest x4 55.6 us: shift(): return lax.ppermute(values, 'seq', pairs)]
    psum x3 -> x0, waiting for transfers between devices: 98.9 us -> none  [the longest x1 50.1 us: per_device(): lax.psum(norm_back(grad_two, unit_two, inverse_two, feedforward_gain), 'mp')]
    pallas_call x0 -> x5, Pallas kernels: none -> 73.4 us  [the longest x1 21.6 us: attend_back(): pl.pallas_call(functools.partial(attend_back_kernel, blocks), grid=(heads...]
    concatenate x1 -> x7, other arithmetic: 0.77 us -> 27.4 us  [the longest x1 16.4 us: per_device(): jnp.concatenate([weight_grad(normed_two, grad_gate), weight_grad(normed_t...]
  transfers between devices with their start and end apart: 21 -> 12, of which waited for: 19 -> 9; matrix products, arithmetic and copies ran while one was open for 9% -> 8% of each run, Pallas kernels for 0% -> 3%
where the time goes in v1:
time: 662 us; the launch traced here: 661 us
  waiting for transfers between devices  435 us (66%)
  Pallas kernels  73.4 us (11%)
  blocking collectives  41.2 us (6%)
  other arithmetic  35.3 us (5%)
  local copies, waits for them, and re-layouts  30.5 us (5%)
  between operations  16.8 us (3%)
  matrix products  15.3 us (2%)
  starting transfers between devices  12.9 us (2%)
    reduce_scatter x1, waiting for transfers between devices, per_device(): lax.psum_scatter(jnp.concatenate([weight_grad(normed_two, grad_gate), wei...  193 us
    all_gather x1, waiting for transfers between devices, per_device(): lax.all_gather(jnp.concatenate([query_weight, key_weight, value_weight, o...  80.2 us
    ppermute x4, waiting for transfers between devices, shift(): return lax.ppermute(values, 'seq', pairs)  55.6 us
    ppermute x4, waiting for transfers between devices, other_half(): lax.ppermute(part, 'mp', [(i, (i + 1) % count) for i in range(count)])  45.3 us
    all_gather x1, waiting for transfers between devices, per_device(): lax.all_gather(jnp.concatenate([gate_weight, up_weight, down_weight], axi...  44.8 us
    psum x1, blocking collectives, per_device(): lax.psum(jnp.concatenate([attention_gain_part[0], feed_gain_part[0], head...  41.2 us
    unnamed x54, local copies, waits for them, and re-layouts  22 us
    pallas_call x1, Pallas kernels, attend_back(): pl.pallas_call(functools.partial(attend_back_kernel, blocks), grid=(heads...  21.6 us
  transfers between devices with their start and end apart: 12, of which 9 were waited for; matrix products, arithmetic and copies ran while one was open for 8% of the time, Pallas kernels for 3%

profile of v1, /device:TPU:0, one launch (start us, length us, event | category | flops | bytes accessed | tf_op | source)
XLA Modules:
  0.0 660.8 jit_solution(2565609953295216021)
XLA Ops:
  9.3 2.4 pad_maximum_fusion.2
  14.4 80.2 %all-gather.3.cloned.1.call-done.w_ref.refs_9_.refs_8_.refs_10_ = bf16[1536,3072]{1,0:T(8,128)(2,1)} async-done(((bf16[96,3072]{1,0:T(8,128)(2,1)}), bf16[1536,3072]{1,0:T(8,128)(2,1)}) %all-gather.3.cloned.1.call-update) | async-done | bytes 9437200 | tf_op jit(solution)/shard_map/all_gather | solution.py:511
  94.5 10.3 %qkv_project.1 = (bf16[256,2304]{1,0:T(8,128)(2,1)}, bf16[256,1536]{1,0:T(8,128)(2,1)}) custom-call(bf16[256,1536]{1,0:T(8,128)(2,1)} %bitcast.37, f32[1,1536]{1,0:T(1,128)} %broadcast_in_dim.53.gain_ref.refs_1_, f32[256,128]{1,0:T(8,128)} %get-tuple-element.153.cos_ref.refs_4_.refs_2_, f32[256,128]{1,0:T(8,128)} %get-tuple-element.154.sin_ref.refs_5_.refs_3_, ...), custom_call_target="tpu_custom_call" | custom-call | flops 1811939328 | bytes 8650752 | tf_op jit(solution)/shard_map/qkv_project/pallas_call | solution.py:74
  106.0 2.4 collective-permute-start.1
  113.8 29.3 %collective-permute-done.1.refs_7_.refs_10_.refs_16_.refs_19_ = bf16[256,1536]{1,0:T(8,128)(2,1)S(1)} collective-permute-done((bf16[256,1536]{1,0:T(8,128)(2,1)S(1)}, bf16[256,1536]{1,0:T(8,128)(2,1)S(1)}, u32[]{:S(2)}, u32[]{:S(2)}) %collective-permute-start.1) | collective-permute-done | bytes 786464 | tf_op jit(solution)/shard_map/ppermute | solution.py:487
  144.3 11.0 %attend_forward.1 = (bf16[256,768]{1,0:T(8,128)(2,1)}, f32[256,768]{1,0:T(8,128)}, f32[256,768]{1,0:T(8,128)}, f32[6,256,2]{2,1,0:T(8,128)}) custom-call(f32[1,1]{1,0:T(1,128)} %bitcast.1.refs_0_, s32[256,1]{1,0:T(8,128)} %copy.53.refs_1_, s32[3,256]{1,0:T(4,128)} %pad_add_fusion.refs_2_, f32[1,128]{1,0:T(1,128)} %bitcast.43, ...), custom_call_target="tpu_custom_call" | custom-call | flops 1207959552 | bytes 4718592 | tf_op jit(solution)/shard_map/attend_forward/pallas_call | solution.py:152
  155.3 2.7 convolution_convert_fusion.7.own_ref
  161.1 9.0 %collective-permute-done.2.other_ref = bf16[256,1536]{1,0:T(8,128)(2,1)S(1)} collective-permute-done((bf16[256,1536]{1,0:T(8,128)(2,1)S(1)}, bf16[256,1536]{1,0:T(8,128)(2,1)S(1)}, u32[]{:S(2)}, u32[]{:S(2)}) %collective-permute-start.2) | collective-permute-done | bytes 786464 | tf_op jit(solution)/shard_map/ppermute | solution.py:481
  170.1 44.8 %all-gather.5.cloned.1.call-done.gate_ref.up_ref.down_ref = bf16[1536,6144]{1,0:T(8,128)(2,1)} async-done(((bf16[96,6144]{1,0:T(8,128)(2,1)}), bf16[1536,6144]{1,0:T(8,128)(2,1)}) %all-gather.5.cloned.1.call-update) | async-done | bytes 18874384 | tf_op jit(solution)/shard_map/all_gather | solution.py:515
  214.9 19.6 %feed_forward.1 = (f32[256,1536]{1,0:T(8,128)}, bf16[256,1536]{1,0:T(8,128)(2,1)}, bf16[256,1536]{1,0:T(8,128)(2,1)}, bf16[256,2048]{1,0:T(8,128)(2,1)}, bf16[25...) custom-call(bf16[256,1536]{1,0:T(8,128)(2,1)} %bitcast.38, ...), custom_call_target="tpu_custom_call" | custom-call | flops 9663676416 | bytes 26738688 | tf_op jit(solution)/shard_map/feed_forward/pallas_call | solution.py:238
  236.3 17.9 %collective-permute-done.4.refs_8_ = bf16[256,1536]{1,0:T(8,128)(2,1)S(1)} collective-permute-done((bf16[256,1536]{1,0:T(8,128)(2,1)}, bf16[256,1536]{1,0:T(8,128)(2,1)S(1)}, u32[]{:S(2)}, u32[]{:S(2)}) %collective-permute-start.4) | collective-permute-done | bytes 786464 | tf_op jit(solution)/shard_map/ppermute | solution.py:481
  255.1 21.6 %attend_backward.1 = (f32[256,1536]{1,0:T(8,128)}, bf16[256,1536]{1,0:T(8,128)(2,1)}, bf16[256,768]{1,0:T(8,128)(2,1)}, f32[256,1536]{1,0:T(8,128)}, bf16[256,15...) custom-call(f32[1,1]{1,0:T(1,128)} %bitcast.1.refs_0_, ...), custom_call_target="tpu_custom_call" | custom-call | flops 4227858432 | bytes 11796480 | tf_op jit(solution)/shard_map/attend_backward/pallas_call | solution.py:345
  284.0 26.3 %collective-permute-done.6.refs_7_ = bf16[256,1536]{1,0:T(8,128)(2,1)} collective-permute-done((bf16[256,1536]{1,0:T(8,128)(2,1)}, bf16[256,1536]{1,0:T(8,128)(2,1)}, u32[]{:S(2)}, u32[]{:S(2)}) %collective-permute-start.6) | collective-permute-done | bytes 786464 | tf_op jit(solution)/shard_map/ppermute | solution.py:487
  310.3 10.8 %input_backward.1 = (bf16[256,768]{1,0:T(8,128)(2,1)}, bf16[256,768]{1,0:T(8,128)(2,1)}, bf16[256,1536]{1,0:T(8,128)(2,1)}, f32[1,1536]{1,0:T(1,128)}) custom-call(bf16[256,1536]{1,0:T(8,128)(2,1)} %bitcast.39, f32[1,1536]{1,0:T(1,128)} %broadcast_in_dim.53.gain_ref.refs_1_, f32[256,128]{1,0:T(8,128)} %get-tuple-element.153.cos_ref.refs_4_.refs_2_, ...), custom_call_target="tpu_custom_call" | custom-call | flops 1811939328 | bytes 13369344 | tf_op jit(solution)/shard_map/input_backward/pallas_call | solution.py:434
  324.7 4.3 pad_maximum_fusion.1
  329.0 12.7 %copy.60 = bf16[1536,3072]{1,0:T(8,128)(2,1)} copy(bf16[1536,3072]{0,1:T(8,128)(2,1)} %pad_maximum_fusion.1) | data formatting | bytes 18874368
  348.8 16.4 %pad_maximum_fusion = bf16[1536,6144]{1,0:T(8,128)(2,1)} fusion(bf16[1536,2048]{1,0:T(8,128)(2,1)S(1)} %convolution_convert_fusion, bf16[1536,2048]{1,0:T(8,128)(2,1)S(1)} %convolution_convert_fusion.1, bf16[1536,2048]{1,0:T(8,128)(2,1)S(1)} %convolution_convert_fusion.2), kind=kLoop, calls=%fused_computation | loop fusion | flops 56623104 | bytes 37748736 | tf_op jit(solution)/shard_map/concatenate | solution.py:566
  367.7 18.4 %collective-permute-done.3 = bf16[256,1536]{1,0:T(8,128)(2,1)} collective-permute-done((bf16[256,1536]{1,0:T(8,128)(2,1)}, bf16[256,1536]{1,0:T(8,128)(2,1)}, u32[]{:S(2)}, u32[]{:S(2)}) %collective-permute-start.3) | collective-permute-done | bytes 786464 | tf_op jit(solution)/shard_map/ppermute | solution.py:481
  386.0 2.5 fusion.1
  389.9 41.2 %psum.7 = f32[3201]{0:T(1024)S(1)} all-reduce(f32[3201]{0:T(1024)S(1)} %pad_maximum_fusion.6), channel_id=1, replica_groups=mesh['dp'=4,'seq'=4,'mp'=2] {'dp','seq','mp'}, use_global_device_ids=true, to_apply=%region_6.7 | all-reduce | flops 3201 | bytes 25608 | tf_op jit(solution)/shard_map/psum | solution.py:594
  434.6 2.5 fusion.2
  437.2 16.7 %reduce-scatter.7.cloned.1.call-done = bf16[96,3072]{1,0:T(8,128)(2,1)} async-done(((bf16[1536,3072]{1,0:T(8,128)(2,1)}), bf16[96,3072]{1,0:T(8,128)(2,1)}) %reduce-scatter.7.cloned.1.call-update) | async-done | bytes 589840
  458.9 192.6 %reduce-scatter.5.cloned.1.call-done = bf16[96,6144]{1,0:T(8,128)(2,1)} async-done(((bf16[1536,6144]{1,0:T(8,128)(2,1)}), bf16[96,6144]{1,0:T(8,128)(2,1)}) %reduce-scatter.5.cloned.1.call-update) | async-done | bytes 1179664 | tf_op jit(solution)/shard_map/reduce_scatter | solution.py:565
  651.6 2.7 fusion.5
  (110 shorter events, 45.5 us)
Async XLA Ops:
  7.2 87.3 %all-gather.3.cloned.1.call-start = ((), (), s32[]{:S(2)}) async-start(), calls=%async_computation.2 | async-start | bytes 10027008 | tf_op jit(solution)/shard_map/all_gather | solution.py:511
  9.2 2.5 copy-start.22
  9.2 2.7 copy-start.16
  9.2 205.6 %all-gather.5.cloned.1.call-start = ((), (), s32[]{:S(2)}) async-start(), calls=%async_computation.3 | async-start | bytes 20054016 | tf_op jit(solution)/shard_map/all_gather | solution.py:515
  11.7 442.2 %reduce-scatter.7.cloned.1.call-start = ((), (), s32[]{:S(2)}) async-start(), calls=%async_computation.5 | async-start | bytes 10027008
  94.5 15.9 %copy-start.18 = (f32[4,64]{1,0:T(4,128)S(1)}, f32[4,64]{1,0:T(4,128)}, u32[]{:S(2)}) copy-start(f32[4,64]{1,0:T(4,128)} %param.22) | copy-start | bytes 3076
  106.0 37.1 %collective-permute-start.1 = (bf16[256,1536]{1,0:T(8,128)(2,1)S(1)}, bf16[256,1536]{1,0:T(8,128)(2,1)S(1)}, u32[]{:S(2)}, u32[]{:S(2)}) collective-permute-start(bf16[256,1536]{1,0:T(8,128)(2,1)S(1)} %slice.60), channel_id=1, source_target_pairs={{0,4},{2,6},{1,5},{3,7},{8,12},{10,14},{9,13},{11,15},{16,20},{18,... | collective-permute-start | bytes 2359304 | tf_op jit(solution)/shard_map/ppermute | solution.py:487
  108.4 34.7 %collective-permute-start = (bf16[256,1536]{1,0:T(8,128)(2,1)S(1)}, bf16[256,1536]{1,0:T(8,128)(2,1)S(1)}, u32[]{:S(2)}, u32[]{:S(2)}) collective-permute-start(bf16[256,1536]{1,0:T(8,128)(2,1)S(1)} %slice.60), channel_id=1, source_target_pairs={{0,2},{2,4},{4,6},{1,3},{3,5},{5,7},{8,10},{10,12},{12,14},{9,11},... | collective-permute-start | bytes 2359304 | tf_op jit(solution)/shard_map/ppermute | solution.py:487
  155.3 4.3 copy-start.17
  158.0 56.8 %copy-start.12 = (bf16[256,1536]{1,0:T(8,128)(2,1)}, bf16[256,1536]{1,0:T(8,128)(2,1)S(1)}, u32[]{:S(2)}) copy-start(bf16[256,1536]{1,0:T(8,128)(2,1)S(1)} %convolution_convert_fusion.7.own_ref) | copy-start | bytes 2359300
  158.0 12.1 %collective-permute-start.2 = (bf16[256,1536]{1,0:T(8,128)(2,1)S(1)}, bf16[256,1536]{1,0:T(8,128)(2,1)S(1)}, u32[]{:S(2)}, u32[]{:S(2)}) collective-permute-start(bf16[256,1536]{1,0:T(8,128)(2,1)S(1)} %convolution_convert_fusion.7.own_ref), channel_id=1, source_target_pairs={{0,1},{1,0},{2,3},{3,2},{4,5},{5,4},{6,7},{7,6},{8,9},{9,8},{10,11... | collective-permute-start | bytes 2359304 | tf_op jit(solution)/shard_map/ppermute | solution.py:481
  170.1 44.8 %copy-start.13 = (bf16[256,1536]{1,0:T(8,128)(2,1)}, bf16[256,1536]{1,0:T(8,128)(2,1)S(1)}, u32[]{:S(2)}) copy-start(bf16[256,1536]{1,0:T(8,128)(2,1)S(1)} %collective-permute-done.2.other_ref) | copy-start | bytes 2359300
  234.5 19.6 %collective-permute-start.4 = (bf16[256,1536]{1,0:T(8,128)(2,1)}, bf16[256,1536]{1,0:T(8,128)(2,1)S(1)}, u32[]{:S(2)}, u32[]{:S(2)}) collective-permute-start(bf16[256,1536]{1,0:T(8,128)(2,1)} %get-tuple-element.45.refs_7_), channel_id=1, source_target_pairs={{0,1},{1,0},{2,3},{3,2},{4,5},{5,4},{6,7},{7,6},{8,9},{9,8},{10,11... | collective-permute-start | bytes 2359304 | tf_op jit(solution)/shard_map/ppermute | solution.py:481
  276.7 7.2 %collective-permute-start.5 = (bf16[256,1536]{1,0:T(8,128)(2,1)}, bf16[256,1536]{1,0:T(8,128)(2,1)}, u32[]{:S(2)}, u32[]{:S(2)}) collective-permute-start(bf16[256,1536]{1,0:T(8,128)(2,1)} %get-tuple-element.52), channel_id=1, source_target_pairs={{2,0},{4,2},{6,4},{3,1},{5,3},{7,5},{10,8},{12,10},{14,12},{11,9},... | collective-permute-start | bytes 2359304 | tf_op jit(solution)/shard_map/ppermute | solution.py:487
  278.0 32.3 %collective-permute-start.6 = (bf16[256,1536]{1,0:T(8,128)(2,1)}, bf16[256,1536]{1,0:T(8,128)(2,1)}, u32[]{:S(2)}, u32[]{:S(2)}) collective-permute-start(bf16[256,1536]{1,0:T(8,128)(2,1)} %get-tuple-element.53), channel_id=1, source_target_pairs={{4,0},{6,2},{5,1},{7,3},{12,8},{14,10},{13,9},{15,11},{20,16},{22,... | collective-permute-start | bytes 2359304 | tf_op jit(solution)/shard_map/ppermute | solution.py:487
  279.5 2.2 copy-start
  341.8 309.8 %reduce-scatter.5.cloned.1.call-start = ((), (), s32[]{:S(2)}) async-start(), calls=%async_computation.4 | async-start | bytes 20054016 | tf_op jit(solution)/shard_map/reduce_scatter | solution.py:565
  365.2 20.9 %copy-start.8 = (f32[256,1536]{1,0:T(8,128)S(1)}, f32[256,1536]{1,0:T(8,128)}, u32[]{:S(2)}) copy-start(f32[256,1536]{1,0:T(8,128)} %get-tuple-element.42) | copy-start | bytes 4718596
  365.2 23.4 %copy-start.23 = (f32[1,128]{1,0:T(1,128)S(1)}, f32[1,128]{1,0:T(1,128)}, u32[]{:S(2)}) copy-start(f32[1,128]{1,0:T(1,128)} %get-tuple-element.58) | copy-start | bytes 1540
  365.2 24.0 %copy-start.20 = (f32[1,1536]{1,0:T(1,128)S(1)}, f32[1,1536]{1,0:T(1,128)}, u32[]{:S(2)}) copy-start(f32[1,1536]{1,0:T(1,128)} %get-tuple-element.55) | copy-start | bytes 18436
  365.2 24.0 %copy-start.21 = (f32[1,128]{1,0:T(1,128)S(1)}, f32[1,128]{1,0:T(1,128)}, u32[]{:S(2)}) copy-start(f32[1,128]{1,0:T(1,128)} %get-tuple-element.57) | copy-start | bytes 1540
  365.2 69.4 %copy-start.7 = (f32[256,1536]{1,0:T(8,128)S(1)}, f32[256,1536]{1,0:T(8,128)}, u32[]{:S(2)}) copy-start(f32[256,1536]{1,0:T(8,128)} %get-tuple-element.49) | copy-start | bytes 4718596
  365.2 20.8 %collective-permute-start.3 = (bf16[256,1536]{1,0:T(8,128)(2,1)}, bf16[256,1536]{1,0:T(8,128)(2,1)}, u32[]{:S(2)}, u32[]{:S(2)}) collective-permute-start(bf16[256,1536]{1,0:T(8,128)(2,1)} %get-tuple-element.43), channel_id=1, source_target_pairs={{0,1},{1,0},{2,3},{3,2},{4,5},{5,4},{6,7},{7,6},{8,9},{9,8},{10,11... | collective-permute-start | bytes 2359304 | tf_op jit(solution)/shard_map/ppermute | solution.py:481
  367.0 67.6 %collective-permute-start.7 = (bf16[256,1536]{1,0:T(8,128)(2,1)}, bf16[256,1536]{1,0:T(8,128)(2,1)}, u32[]{:S(2)}, u32[]{:S(2)}) collective-permute-start(bf16[256,1536]{1,0:T(8,128)(2,1)} %get-tuple-element.54), channel_id=1, source_target_pairs={{0,1},{1,0},{2,3},{3,2},{4,5},{5,4},{6,7},{7,6},{8,9},{9,8},{10,11... | collective-permute-start | bytes 2359304 | tf_op jit(solution)/shard_map/ppermute | solution.py:481
  (12 other events, 18.7 us)
Sparse Core Ops, SparseCore 0:
  10.8 83.6 all-gather.2
  96.1 118.7 all-gather.4
  341.9 111.9 reduce-scatter.6
  457.9 193.6 reduce-scatter.4

commit v2 on v1

--- a/solution.py
+++ b/solution.py
@@ -487,8 +487,116 @@
     return lax.ppermute(values, "seq", pairs)
 
 
-def weight_grad(left, right):
-    return dot_tn(left, right).astype(BF16)
+def flip(values, bit):
+    count = lax.axis_size("seq")
+    return lax.ppermute(values, "seq", [(i, i ^ bit) for i in range(count)])
+
+
+def everyone_sum(values):
+    for axis in ("mp", "seq", "dp"):
+        count = lax.axis_size(axis)
+        if count & (count - 1):
+            values = lax.psum(values, axis)
+            continue
+        bit = 1
+        while bit < count:
+            values = values + lax.ppermute(values, axis, [(i, i ^ bit) for i in range(count)])
+            bit *= 2
+    return values
+
+
+def split_grad_kernel(counts, dp_count, dp_major, rows, me_ref, *refs):
+    pairs = len(counts)
+    lefts, rights = refs[:pairs], refs[pairs : 2 * pairs]
+    send_ref, keep_ref = refs[2 * pairs :]
+    step = pl.program_id(0)
+    core = me_ref[0, 0] % 2
+    side = (me_ref[0, 0] // 2) % 2
+    start = 0
+    for left_ref, right_ref, count in zip(lefts, rights, counts):
+
+        @pl.when((step >= start) & (step < start + count))
+        def _(left_ref=left_ref, right_ref=right_ref):
+            product = dot_tn(left_ref[...], right_ref[...]).astype(BF16)
+            for d in range(dp_count):
+                for x in range(2):
+                    first = (d * 4 + x * 2) * rows
+                    even = product[first : first + rows]
+                    odd = product[first + rows : first + 2 * rows]
+                    mine = (side == x).astype(jnp.int32)
+                    if dp_major:
+                        place = (2 * d + mine) * rows
+                    else:
+                        place = (mine * dp_count + d) * rows
+                    spot = pl.ds(pl.multiple_of(place, rows), rows)
+                    send_ref[spot, :] = jnp.where(core == 0, odd, even)
+                    keep_ref[spot, :] = jnp.where(core == 0, even, odd)
+
+        start += count
+
+
+def split_grads(me, pairs, dp_count, dp_major):
+    length, model = pairs[0][0].shape
+    tile = 256
+    counts = tuple(right.shape[1] // tile for _, right in pairs)
+    starts = [sum(counts[:i]) for i in range(len(counts))]
+    width = tile * sum(counts)
+    rows = model // (4 * dp_count)
+
+    def right_spec(start, count):
+        return pl.BlockSpec((length, tile), lambda j: (0, jnp.clip(j - start, 0, count - 1)))
+
+    column = pl.BlockSpec((model // 2, tile), lambda j: (0, j))
+    return pl.pallas_call(
+        functools.partial(split_grad_kernel, counts, dp_count, dp_major, rows),
+        grid=(sum(counts),),
+        in_specs=[
+            pl.BlockSpec(memory_space=pltpu.SMEM),
+            *[full_spec((length, model)) for _ in pairs],
+            *[right_spec(start, count) for start, count in zip(starts, counts)],
+        ],
+        out_specs=[column, column],
+        out_shape=[jax.ShapeDtypeStruct((model // 2, width), BF16)] * 2,
+        cost_estimate=cost(2 * length * model * width, 2 * model * width + 4 * length * width),
+        name="weight_grads",
+    )(me, *[left for left, _ in pairs], *[right for _, right in pairs])
+
+
+def add(first, second):
+    return first.astype(F32) + second.astype(F32)
+
+
+def staged_scatter(me, pairs, order):
+    dp_count = lax.axis_size("dp")
+    send, keep = split_grads(me.reshape(1, 1), pairs, dp_count, order == "dp_first")
+    arrived = flip(send, 1)
+    if order == "dp_first":
+        total = lax.psum_scatter(
+            add(keep, arrived).astype(BF16), "dp", scatter_dimension=0, tiled=True
+        )
+        half = total.shape[0] // 2
+        return add(total[half:], flip(total[:half], 2))
+    half = keep.shape[0] // 2
+    away = flip(add(keep[:half], arrived[:half]).astype(BF16), 2)
+    total = add(keep[half:], arrived[half:]) + away.astype(F32)
+    if order == "queue":
+        total = total.astype(BF16)
+        return lax.psum_scatter(total, "dp", scatter_dimension=0, tiled=True).astype(F32)
+    by_owner = total.astype(BF16).reshape(dp_count, half // dp_count, -1)
+    place = lax.axis_index("dp")
+    result = lax.dynamic_index_in_dim(by_owner, place, 0, keepdims=False).astype(F32)
+    for step in range(1, dp_count):
+        chunk = lax.dynamic_index_in_dim(by_owner, (place + step) % dp_count, 0, keepdims=False)
+        hops = [(i, (i + step) % dp_count) for i in range(dp_count)]
+        result = result + lax.ppermute(chunk, "dp", hops).astype(F32)
+    return result
+
+
+def plain_scatter(pairs):
+    grads = [dot_tn(left, right).astype(BF16) for left, right in pairs]
+    return lax.psum_scatter(
+        jnp.concatenate(grads, axis=1), ("dp", "seq"), scatter_dimension=0, tiled=True
+    ).astype(F32)
 
 
 def per_device(
@@ -562,46 +670,27 @@
     prior_kv = outs[4 : 4 + back_steps]
     head_gain_part, lambda_part = outs[4 + back_steps :]
     result = hidden + (feed_part.astype(F32) + other_half(feed_part).astype(F32))
-    feed_grads = lax.psum_scatter(
-        jnp.concatenate(
-            [
-                weight_grad(normed_two, grad_gate),
-                weight_grad(normed_two, grad_up),
-                weight_grad(grad_low, inner),
-            ],
-            axis=1,
-        ),
-        whole, scatter_dimension=0, tiled=True,
-    ).astype(F32)
+    model = inputs.shape[1]
+    staged = seq_count == 4 and model % (32 * 4 * lax.axis_size("dp")) == 0
+
+    def scatter(pairs, order):
+        return staged_scatter(me, pairs, order) if staged else plain_scatter(pairs)
+
+    down_grad = scatter([(grad_low, inner)], "direct")
+    up_grad = scatter([(normed_two, grad_up)], "queue")
+    gate_grad = scatter([(normed_two, grad_gate)], "dp_first")
+    query_out_grad = scatter([(normed_one, grad_q), (hidden_low, normed_head)], "queue")
     arrived = [shift(values, -(b + 1)) for b, values in enumerate(prior_kv)]
     grad_k, grad_v, input_part, attention_gain_part = input_back(
         inputs, gain_one, cos_table, sin_table, grad_q, own_kv, arrived, attention_weights, heads,
         head_width,
     )
-    attention_grads = lax.psum_scatter(
-        jnp.concatenate(
-            [
-                weight_grad(normed_one, grad_q),
-                weight_grad(normed_one, grad_k),
-                weight_grad(normed_one, grad_v),
-                weight_grad(hidden_low, normed_head),
-            ],
-            axis=1,
-        ),
-        whole, scatter_dimension=0, tiled=True,
-    ).astype(F32)
+    key_value_grad = scatter([(normed_one, grad_k), (normed_one, grad_v)], "direct")
     grad_tokens = grad_hidden + (input_part.astype(F32) + other_half(input_part).astype(F32))
-    gain_sums = lax.psum(
-        jnp.concatenate(
-            [
-                attention_gain_part[0], feed_gain_part[0], head_gain_part[0],
-                jnp.sum(lambda_part).reshape(1),
-            ]
-        ),
-        ("dp", "seq", "mp"),
-    )
-    model = inputs.shape[1]
-    lambda_total = gain_sums[-1]
+    gain_sums = everyone_sum(
+        jnp.concatenate([attention_gain_part, feed_gain_part, head_gain_part, lambda_part], axis=1)
+    )[0]
+    lambda_total = jnp.sum(gain_sums[-head_width:])
     lambda_grad = jnp.stack(
         [
             lambda_total * first_exp * lambda_vectors[1],
@@ -614,16 +703,16 @@
         result.astype(BF16)[None],
         grad_tokens.astype(BF16)[None],
         gain_sums[:model],
-        attention_grads[:, :width],
-        attention_grads[:, width : 2 * width],
-        attention_grads[:, 2 * width : 3 * width],
-        attention_grads[:, 3 * width :],
+        query_out_grad[:, :width],
+        key_value_grad[:, :width],
+        key_value_grad[:, width:],
+        query_out_grad[:, width:],
         gain_sums[2 * model : 2 * model + head_width],
         lambda_grad,
         gain_sums[model : 2 * model],
-        feed_grads[:, :hidden_units],
-        feed_grads[:, hidden_units : 2 * hidden_units],
-        feed_grads[:, 2 * hidden_units :],
+        gate_grad,
+        up_grad,
+        down_grad,
     )
 
 

time: 662 us -> 547 us (0.83)
  waiting for transfers between devices: 435 us -> 313 us
  blocking collectives: 41.2 us -> 0 us
  Pallas kernels: 73.4 us -> 111 us
  starting transfers between devices: 12.9 us -> 38 us
  local copies, waits for them, and re-layouts: 30.5 us -> 13.8 us
  matrix products: 15.3 us -> 2.61 us
  other arithmetic: 35.3 us -> 45.6 us
    reduce_scatter x1 -> x3, waiting for transfers between devices: 193 us -> 0.02 us  [the longest x1 0.02 us: staged_scatter(): lax.psum_scatter(add(keep, arrived).astype(BF16), 'dp', scatter_dimension...]
    ppermute x0 -> x21, waiting for transfers between devices: none -> 120 us  [the longest x10 88.9 us: flip(): return lax.ppermute(values, 'seq', [(i, i ^ bit) for i in range(count)])]
    psum x1 -> x0, blocking collectives: 41.2 us -> none  [per_device(): lax.psum(jnp.concatenate([attention_gain_part[0], feed_gain_part[0], head...]
    pallas_call x0 -> x5, Pallas kernels: none -> 37.9 us  [split_grads(): pl.pallas_call(functools.partial(split_grad_kernel, counts, dp_count, dp_...]
    convert_element_type x0 -> x10, other arithmetic: none -> 29.2 us  [the longest x4 12 us: staged_scatter(): away = flip(add(keep[:half], arrived[:half]).astype(BF16), 2)]
    ppermute x0 -> x21, starting transfers between devices: none -> 23.8 us  [the longest x6 12.8 us: staged_scatter(): result = result + lax.ppermute(chunk, 'dp', hops).astype(F32)]
    concatenate x3 -> x0, other arithmetic: 21.4 us -> none  [the longest x1 16.4 us: per_device(): jnp.concatenate([weight_grad(normed_two, grad_gate), weight_grad(normed_t...]
    ppermute x4, waiting for transfers between devices: 45.3 us -> 26.9 us  [other_half(): lax.ppermute(part, 'mp', [(i, (i + 1) % count) for i in range(count)])]
  transfers between devices with their start and end apart: 12 -> 34, of which waited for: 9 -> 18; matrix products, arithmetic and copies ran while one was open for 8% -> 9% of each run, Pallas kernels for 3% -> 15%
where the time goes in v2:
time: 547 us; the launch traced here: 542 us
  waiting for transfers between devices  313 us (57%)
  Pallas kernels  111 us (20%)
  other arithmetic  45.6 us (8%)
  starting transfers between devices  38 us (7%)
  between operations  16.9 us (3%)
  local copies, waits for them, and re-layouts  13.8 us (3%)
    ppermute x10, waiting for transfers between devices, flip(): return lax.ppermute(values, 'seq', [(i, i ^ bit) for i in range(count)])  88.9 us
    all_gather x1, waiting for transfers between devices, per_device(): lax.all_gather(jnp.concatenate([query_weight, key_weight, value_weight, o...  80.2 us
    all_gather x1, waiting for transfers between devices, per_device(): lax.all_gather(jnp.concatenate([gate_weight, up_weight, down_weight], axi...  43.1 us
    ppermute x4, waiting for transfers between devices, shift(): return lax.ppermute(values, 'seq', pairs)  42.9 us
    pallas_call x5, Pallas kernels, split_grads(): pl.pallas_call(functools.partial(split_grad_kernel, counts, dp_count, dp_...  37.9 us
    ppermute x4, waiting for transfers between devices, other_half(): lax.ppermute(part, 'mp', [(i, (i + 1) % count) for i in range(count)])  26.9 us
    ppermute x6, waiting for transfers between devices, staged_scatter(): result = result + lax.ppermute(chunk, 'dp', hops).astype(F32)  24.4 us
    pallas_call x1, Pallas kernels, attend_back(): pl.pallas_call(functools.partial(attend_back_kernel, blocks), grid=(heads...  21.7 us
  transfers between devices with their start and end apart: 34, of which 18 were waited for; matrix products, arithmetic and copies ran while one was open for 9% of the time, Pallas kernels for 15%

profile of v2, /device:TPU:0, one launch (start us, length us, event | category | flops | bytes accessed | tf_op | source)
XLA Modules:
  0.0 541.6 jit_solution(7712513758604410232)
XLA Ops:
  14.3 80.2 %all-gather.3.cloned.1.call-done.w_ref.refs_9_.refs_8_.refs_10_ = bf16[1536,3072]{1,0:T(8,128)(2,1)} async-done(((bf16[96,3072]{1,0:T(8,128)(2,1)}), bf16[1536,3072]{1,0:T(8,128)(2,1)}) %all-gather.3.cloned.1.call-update) | async-done | bytes 9437200 | tf_op jit(solution)/shard_map/all_gather | solution.py:619
  94.5 10.3 %qkv_project.1 = (bf16[256,2304]{1,0:T(8,128)(2,1)}, bf16[256,1536]{1,0:T(8,128)(2,1)}) custom-call(bf16[256,1536]{1,0:T(8,128)(2,1)} %bitcast.42, f32[1,1536]{1,0:T(1,128)} %broadcast_in_dim.53.gain_ref.refs_1_, f32[256,128]{1,0:T(8,128)} %get-tuple-element.113.cos_ref.refs_4_.refs_2_, f32[256,128]{1,0:T(8,128)} %get-tuple-element.114.sin_ref.refs_5_.refs_3_, ...), custom_call_target="tpu_custom_call" | custom-call | flops 1811939328 | bytes 8650752 | tf_op jit(solution)/shard_map/qkv_project/pallas_call | solution.py:74
  114.1 31.2 %collective-permute-done.1.refs_7_.refs_10_.refs_16_.refs_19_ = bf16[256,1536]{1,0:T(8,128)(2,1)S(1)} collective-permute-done((bf16[256,1536]{1,0:T(8,128)(2,1)S(1)}, bf16[256,1536]{1,0:T(8,128)(2,1)S(1)}, u32[]{:S(2)}, u32[]{:S(2)}) %collective-permute-start.1) | collective-permute-done | bytes 786464 | tf_op jit(solution)/shard_map/ppermute | solution.py:487
  146.1 10.9 %attend_forward.1 = (bf16[256,768]{1,0:T(8,128)(2,1)}, f32[256,768]{1,0:T(8,128)}, f32[256,768]{1,0:T(8,128)}, f32[6,256,2]{2,1,0:T(8,128)}) custom-call(f32[1,1]{1,0:T(1,128)} %bitcast.1.refs_0_, s32[256,1]{1,0:T(8,128)} %copy.34.refs_1_, s32[3,256]{1,0:T(4,128)} %pad_add_fusion.refs_2_, f32[1,128]{1,0:T(1,128)} %bitcast.52, ...), custom_call_target="tpu_custom_call" | custom-call | flops 1207959552 | bytes 4718592 | tf_op jit(solution)/shard_map/attend_forward/pallas_call | solution.py:152
  162.7 9.0 %collective-permute-done.2.other_ref = bf16[256,1536]{1,0:T(8,128)(2,1)S(1)} collective-permute-done((bf16[256,1536]{1,0:T(8,128)(2,1)S(1)}, bf16[256,1536]{1,0:T(8,128)(2,1)S(1)}, u32[]{:S(2)}, u32[]{:S(2)}) %collective-permute-start.2) | collective-permute-done | bytes 786464 | tf_op jit(solution)/shard_map/ppermute | solution.py:481
  171.8 43.1 %all-gather.5.cloned.1.call-done.gate_ref.up_ref.down_ref = bf16[1536,6144]{1,0:T(8,128)(2,1)} async-done(((bf16[96,6144]{1,0:T(8,128)(2,1)}), bf16[1536,6144]{1,0:T(8,128)(2,1)}) %all-gather.5.cloned.1.call-update) | async-done | bytes 18874384 | tf_op jit(solution)/shard_map/all_gather | solution.py:623
  214.8 19.7 %feed_forward.1 = (f32[256,1536]{1,0:T(8,128)}, bf16[256,1536]{1,0:T(8,128)(2,1)}, bf16[256,1536]{1,0:T(8,128)(2,1)}, bf16[256,2048]{1,0:T(8,128)(2,1)}, bf16[25...) custom-call(bf16[256,1536]{1,0:T(8,128)(2,1)} %bitcast.43, ...), custom_call_target="tpu_custom_call" | custom-call | flops 9663676416 | bytes 26738688 | tf_op jit(solution)/shard_map/feed_forward/pallas_call | solution.py:238
  234.6 8.2 %weight_grads.7 = (bf16[768,2048]{1,0:T(8,128)(2,1)}, bf16[768,2048]{1,0:T(8,128)(2,1)}) custom-call(s32[1,1]{1,0:T(1,128)} %bitcast.12.me_ref, bf16[256,1536]{1,0:T(8,128)(2,1)} %get-tuple-element.77.refs_0_, bf16[256,2048]{1,0:T(8,128)(2,1)} %get-tuple-element.78.refs_1_), custom_call_target="tpu_custom_call" | custom-call | flops 1610612736 | bytes 8388608 | tf_op jit(solution)/shard_map/weight_grads/pallas_call | solution.py:550
  242.7 5.9 %collective-permute-done.20 = bf16[768,2048]{1,0:T(8,128)(2,1)S(1)} collective-permute-done((bf16[768,2048]{1,0:T(8,128)(2,1)}, bf16[768,2048]{1,0:T(8,128)(2,1)S(1)}, u32[]{:S(2)}, u32[]{:S(2)}) %collective-permute-start.20) | collective-permute-done | bytes 3145760 | tf_op jit(solution)/shard_map/ppermute | solution.py:492
  248.6 4.9 add_convert_fusion
  256.3 17.9 %collective-permute-done.4.refs_8_ = bf16[256,1536]{1,0:T(8,128)(2,1)S(1)} collective-permute-done((bf16[256,1536]{1,0:T(8,128)(2,1)S(1)}, bf16[256,1536]{1,0:T(8,128)(2,1)S(1)}, u32[]{:S(2)}, u32[]{:S(2)}) %collective-permute-start.4) | collective-permute-done | bytes 786464 | tf_op jit(solution)/shard_map/ppermute | solution.py:481
  275.1 21.7 %attend_backward.1 = (f32[256,1536]{1,0:T(8,128)}, bf16[256,1536]{1,0:T(8,128)(2,1)}, bf16[256,768]{1,0:T(8,128)(2,1)}, f32[256,1536]{1,0:T(8,128)}, bf16[256,15...) custom-call(f32[1,1]{1,0:T(1,128)} %bitcast.1.refs_0_, ...), custom_call_target="tpu_custom_call" | custom-call | flops 4227858432 | bytes 11796480 | tf_op jit(solution)/shard_map/attend_backward/pallas_call | solution.py:345
  296.8 6.7 %weight_grads.5 = (bf16[768,1536]{1,0:T(8,128)(2,1)}, bf16[768,1536]{1,0:T(8,128)(2,1)}) custom-call(s32[1,1]{1,0:T(1,128)} %bitcast.12.me_ref, bf16[256,1536]{1,0:T(8,128)(2,1)} %get-tuple-element.69.refs_0_.refs_1_, bf16[256,1536]{1,0:T(8,128)(2,1)} %get-tuple-element.70.refs_1_, bf16[256,768]{1,0:T(8,128)(2,1)} %get-tuple-element.60.refs_4_.refs_2_, ...), custom_call_target="tpu_custom_call" | custom-call | flops 1207959552 | bytes 6291456 | tf_op jit(solution)/shard_map/weight_grads/pallas_call | solution.py:550
  306.1 8.1 %weight_grads.9 = (bf16[768,2048]{1,0:T(8,128)(2,1)}, bf16[768,2048]{1,0:T(8,128)(2,1)}) custom-call(s32[1,1]{1,0:T(1,128)} %bitcast.12.me_ref, bf16[256,1536]{1,0:T(8,128)(2,1)} %get-tuple-element.54.refs_6_.refs_0_, bf16[256,2048]{1,0:T(8,128)(2,1)} %get-tuple-element.84.refs_1_), custom_call_target="tpu_custom_call" | custom-call | flops 1610612736 | bytes 8388608 | tf_op jit(solution)/shard_map/weight_grads/pallas_call | solution.py:550
  315.3 8.2 %weight_grads.8 = (bf16[768,2048]{1,0:T(8,128)(2,1)}, bf16[768,2048]{1,0:T(8,128)(2,1)}) custom-call(s32[1,1]{1,0:T(1,128)} %bitcast.12.me_ref, bf16[256,1536]{1,0:T(8,128)(2,1)} %get-tuple-element.77.refs_0_, bf16[256,2048]{1,0:T(8,128)(2,1)} %get-tuple-element.81.refs_1_), custom_call_target="tpu_custom_call" | custom-call | flops 1610612736 | bytes 8388608 | tf_op jit(solution)/shard_map/weight_grads/pallas_call | solution.py:550
  325.2 11.7 %collective-permute-done.6.refs_7_ = bf16[256,1536]{1,0:T(8,128)(2,1)} collective-permute-done((bf16[256,1536]{1,0:T(8,128)(2,1)}, bf16[256,1536]{1,0:T(8,128)(2,1)}, u32[]{:S(2)}, u32[]{:S(2)}) %collective-permute-start.6) | collective-permute-done | bytes 786464 | tf_op jit(solution)/shard_map/ppermute | solution.py:487
  336.9 10.8 %input_backward.1 = (bf16[256,768]{1,0:T(8,128)(2,1)}, bf16[256,768]{1,0:T(8,128)(2,1)}, bf16[256,1536]{1,0:T(8,128)(2,1)}, f32[1,1536]{1,0:T(1,128)}) custom-call(bf16[256,1536]{1,0:T(8,128)(2,1)} %bitcast.44, f32[1,1536]{1,0:T(1,128)} %broadcast_in_dim.53.gain_ref.refs_1_, f32[256,128]{1,0:T(8,128)} %get-tuple-element.113.cos_ref.refs_4_.refs_2_, ...), custom_call_target="tpu_custom_call" | custom-call | flops 1811939328 | bytes 13369344 | tf_op jit(solution)/shard_map/input_backward/pallas_call | solution.py:434
  366.7 6.7 %weight_grads.6 = (bf16[768,1536]{1,0:T(8,128)(2,1)}, bf16[768,1536]{1,0:T(8,128)(2,1)}) custom-call(s32[1,1]{1,0:T(1,128)} %bitcast.12.me_ref, bf16[256,1536]{1,0:T(8,128)(2,1)} %get-tuple-element.69.refs_0_.refs_1_, bf16[256,1536]{1,0:T(8,128)(2,1)} %get-tuple-element.69.refs_0_.refs_1_, bf16[256,768]{1,0:T(8,128)(2,1)} %get-tuple-element.73.refs_2_, ...), custom_call_target="tpu_custom_call" | custom-call | flops 1207959552 | bytes 6291456 | tf_op jit(solution)/shard_map/weight_grads/pallas_call | solution.py:550
  378.7 8.9 %collective-permute-done.14 = bf16[384,1536]{1,0:T(8,128)(2,1)} collective-permute-done((bf16[384,1536]{1,0:T(8,128)(2,1)}, bf16[384,1536]{1,0:T(8,128)(2,1)}, u32[]{:S(2)}, u32[]{:S(2)}) %collective-permute-start.14) | collective-permute-done | bytes 1179680 | tf_op jit(solution)/shard_map/ppermute | solution.py:492
  407.1 26.1 %collective-permute-done.23 = bf16[384,2048]{1,0:T(8,128)(2,1)S(1)} collective-permute-done((bf16[384,2048]{1,0:T(8,128)(2,1)S(1)}, bf16[384,2048]{1,0:T(8,128)(2,1)S(1)}, u32[]{:S(2)}, u32[]{:S(2)}) %collective-permute-start.23) | collective-permute-done | bytes 1572896 | tf_op jit(solution)/shard_map/ppermute | solution.py:492
  435.3 31.7 %collective-permute-done.25 = bf16[384,2048]{1,0:T(8,128)(2,1)} collective-permute-done((bf16[384,2048]{1,0:T(8,128)(2,1)}, bf16[384,2048]{1,0:T(8,128)(2,1)}, u32[]{:S(2)}, u32[]{:S(2)}) %collective-permute-start.25) | collective-permute-done | bytes 1572896 | tf_op jit(solution)/shard_map/ppermute | solution.py:492
  476.4 13.1 %collective-permute-done.16 = bf16[384,1536]{1,0:T(8,128)(2,1)} collective-permute-done((bf16[384,1536]{1,0:T(8,128)(2,1)}, bf16[384,1536]{1,0:T(8,128)(2,1)}, u32[]{:S(2)}, u32[]{:S(2)}) %collective-permute-start.16) | collective-permute-done | bytes 1179680 | tf_op jit(solution)/shard_map/ppermute | solution.py:492
  499.8 5.3 collective-permute-done.17
  505.1 18.3 %collective-permute-done.18 = bf16[96,1536]{1,0:T(8,128)(2,1)S(1)} collective-permute-done((bf16[96,1536]{1,0:T(8,128)(2,1)S(1)}, bf16[96,1536]{1,0:T(8,128)(2,1)S(1)}, u32[]{:S(2)}, u32[]{:S(2)}) %collective-permute-start.18) | collective-permute-done | bytes 294944 | tf_op jit(solution)/shard_map/ppermute | solution.py:591
  (164 shorter events, 106.1 us)
Async XLA Ops:
  7.2 87.3 %all-gather.3.cloned.1.call-start = ((), (), s32[]{:S(2)}) async-start(), calls=%async_computation.3 | async-start | bytes 10027008 | tf_op jit(solution)/shard_map/all_gather | solution.py:619
  9.2 205.6 %all-gather.5.cloned.1.call-start = ((), (), s32[]{:S(2)}) async-start(), calls=%async_computation.4 | async-start | bytes 20054016 | tf_op jit(solution)/shard_map/all_gather | solution.py:623
  11.7 511.9 %reduce-scatter.6.cloned.1.call-start = ((), (), s32[]{:S(2)}) async-start(), calls=%async_computation.6 | async-start | bytes 3932160 | tf_op jit(solution)/shard_map/reduce_scatter | solution.py:574
  108.2 37.0 %collective-permute-start.1 = (bf16[256,1536]{1,0:T(8,128)(2,1)S(1)}, bf16[256,1536]{1,0:T(8,128)(2,1)S(1)}, u32[]{:S(2)}, u32[]{:S(2)}) collective-permute-start(bf16[256,1536]{1,0:T(8,128)(2,1)S(1)} %slice.115), channel_id=1, source_target_pairs={{0,4},{2,6},{1,5},{3,7},{8,12},{10,14},{9,13},{11,15},{16,20},{18,... | collective-permute-start | bytes 2359304 | tf_op jit(solution)/shard_map/ppermute | solution.py:487
  253.5 273.6 %reduce-scatter.4.cloned.1.call-start = ((), (), s32[]{:S(2)}) async-start(), calls=%async_computation.5 | async-start | bytes 1474560 | tf_op jit(solution)/shard_map/reduce_scatter | solution.py:584
  254.6 19.6 %collective-permute-start.4 = (bf16[256,1536]{1,0:T(8,128)(2,1)S(1)}, bf16[256,1536]{1,0:T(8,128)(2,1)S(1)}, u32[]{:S(2)}, u32[]{:S(2)}) collective-permute-start(bf16[256,1536]{1,0:T(8,128)(2,1)S(1)} %copy-done.12), channel_id=1, source_target_pairs={{0,1},{1,0},{2,3},{3,2},{4,5},{5,4},{6,7},{7,6},{8,9},{9,8},{10,11... | collective-permute-start | bytes 2359304 | tf_op jit(solution)/shard_map/ppermute | solution.py:481
  303.5 53.9 %collective-permute-start.13 = (bf16[768,1536]{1,0:T(8,128)(2,1)}, bf16[768,1536]{1,0:T(8,128)(2,1)}, u32[]{:S(2)}, u32[]{:S(2)}) collective-permute-start(bf16[768,1536]{1,0:T(8,128)(2,1)} %get-tuple-element.72), channel_id=1, source_target_pairs={{0,2},{2,0},{4,6},{6,4},{1,3},{3,1},{5,7},{7,5},{8,10},{10,8},{12,... | collective-permute-start | bytes 7077896 | tf_op jit(solution)/shard_map/ppermute | solution.py:492
  303.5 20.0 %collective-permute-start.5 = (bf16[256,1536]{1,0:T(8,128)(2,1)}, bf16[256,1536]{1,0:T(8,128)(2,1)}, u32[]{:S(2)}, u32[]{:S(2)}) collective-permute-start(bf16[256,1536]{1,0:T(8,128)(2,1)} %get-tuple-element.62), channel_id=1, source_target_pairs={{2,0},{4,2},{6,4},{3,1},{5,3},{7,5},{10,8},{12,10},{14,12},{11,9},... | collective-permute-start | bytes 2359304 | tf_op jit(solution)/shard_map/ppermute | solution.py:487
  304.8 32.1 %collective-permute-start.6 = (bf16[256,1536]{1,0:T(8,128)(2,1)}, bf16[256,1536]{1,0:T(8,128)(2,1)}, u32[]{:S(2)}, u32[]{:S(2)}) collective-permute-start(bf16[256,1536]{1,0:T(8,128)(2,1)} %get-tuple-element.63), channel_id=1, source_target_pairs={{4,0},{6,2},{5,1},{7,3},{12,8},{14,10},{13,9},{15,11},{20,16},{22,... | collective-permute-start | bytes 2359304 | tf_op jit(solution)/shard_map/ppermute | solution.py:487
  314.2 82.0 %collective-permute-start.24 = (bf16[768,2048]{1,0:T(8,128)(2,1)}, bf16[768,2048]{1,0:T(8,128)(2,1)}, u32[]{:S(2)}, u32[]{:S(2)}) collective-permute-start(bf16[768,2048]{1,0:T(8,128)(2,1)} %get-tuple-element.86), channel_id=1, source_target_pairs={{0,2},{2,0},{4,6},{6,4},{1,3},{3,1},{5,7},{7,5},{8,10},{10,8},{12,... | collective-permute-start | bytes 9437192 | tf_op jit(solution)/shard_map/ppermute | solution.py:492
  323.5 68.0 %collective-permute-start.22 = (bf16[768,2048]{1,0:T(8,128)(2,1)}, bf16[768,2048]{1,0:T(8,128)(2,1)S(1)}, u32[]{:S(2)}, u32[]{:S(2)}) collective-permute-start(bf16[768,2048]{1,0:T(8,128)(2,1)} %get-tuple-element.83), channel_id=1, source_target_pairs={{0,2},{2,0},{4,6},{6,4},{1,3},{3,1},{5,7},{7,5},{8,10},{10,8},{12,... | collective-permute-start | bytes 9437192 | tf_op jit(solution)/shard_map/ppermute | solution.py:492
  323.5 37.0 %collective-permute-start.3 = (bf16[256,1536]{1,0:T(8,128)(2,1)}, bf16[256,1536]{1,0:T(8,128)(2,1)}, u32[]{:S(2)}, u32[]{:S(2)}) collective-permute-start(bf16[256,1536]{1,0:T(8,128)(2,1)} %get-tuple-element.53), channel_id=1, source_target_pairs={{0,1},{1,0},{2,3},{3,2},{4,5},{5,4},{6,7},{7,6},{8,9},{9,8},{10,11... | collective-permute-start | bytes 2359304 | tf_op jit(solution)/shard_map/ppermute | solution.py:481
  360.4 27.2 %collective-permute-start.14 = (bf16[384,1536]{1,0:T(8,128)(2,1)}, bf16[384,1536]{1,0:T(8,128)(2,1)}, u32[]{:S(2)}, u32[]{:S(2)}) collective-permute-start(bf16[384,1536]{1,0:T(8,128)(2,1)} %add_convert_fusion.8), channel_id=1, source_target_pairs={{0,4},{2,6},{4,0},{6,2},{1,5},{3,7},{5,1},{7,3},{8,12},{10,14},{12... | collective-permute-start | bytes 3538952 | tf_op jit(solution)/shard_map/ppermute | solution.py:492
  373.5 30.5 %collective-permute-start.15 = (bf16[768,1536]{1,0:T(8,128)(2,1)}, bf16[768,1536]{1,0:T(8,128)(2,1)}, u32[]{:S(2)}, u32[]{:S(2)}) collective-permute-start(bf16[768,1536]{1,0:T(8,128)(2,1)} %get-tuple-element.76), channel_id=1, source_target_pairs={{0,2},{2,0},{4,6},{6,4},{1,3},{3,1},{5,7},{7,5},{8,10},{10,8},{12,... | collective-permute-start | bytes 7077896 | tf_op jit(solution)/shard_map/ppermute | solution.py:492
  373.5 28.0 %collective-permute-start.7 = (bf16[256,1536]{1,0:T(8,128)(2,1)}, bf16[256,1536]{1,0:T(8,128)(2,1)}, u32[]{:S(2)}, u32[]{:S(2)}) collective-permute-start(bf16[256,1536]{1,0:T(8,128)(2,1)} %get-tuple-element.64), channel_id=1, source_target_pairs={{0,1},{1,0},{2,3},{3,2},{4,5},{5,4},{6,7},{7,6},{8,9},{9,8},{10,11... | collective-permute-start | bytes 2359304 | tf_op jit(solution)/shard_map/ppermute | solution.py:481
  391.2 137.8 %reduce-scatter.8.cloned.1.call-start = ((), (), s32[]{:S(2)}) async-start(), calls=%async_computation.7 | async-start | bytes 1966080 | tf_op jit(solution)/shard_map/reduce_scatter | solution.py:584
  395.9 37.3 %collective-permute-start.23 = (bf16[384,2048]{1,0:T(8,128)(2,1)S(1)}, bf16[384,2048]{1,0:T(8,128)(2,1)S(1)}, u32[]{:S(2)}, u32[]{:S(2)}) collective-permute-start(bf16[384,2048]{1,0:T(8,128)(2,1)S(1)} %add_convert_fusion.4), channel_id=1, source_target_pairs={{0,4},{2,6},{4,0},{6,2},{1,5},{3,7},{5,1},{7,3},{8,12},{10,14},{12... | collective-permute-start | bytes 4718600 | tf_op jit(solution)/shard_map/ppermute | solution.py:492
  399.8 67.2 %collective-permute-start.25 = (bf16[384,2048]{1,0:T(8,128)(2,1)}, bf16[384,2048]{1,0:T(8,128)(2,1)}, u32[]{:S(2)}, u32[]{:S(2)}) collective-permute-start(bf16[384,2048]{1,0:T(8,128)(2,1)} %add_convert_fusion.2), channel_id=1, source_target_pairs={{0,4},{2,6},{4,0},{6,2},{1,5},{3,7},{5,1},{7,3},{8,12},{10,14},{12... | collective-permute-start | bytes 4718600 | tf_op jit(solution)/shard_map/ppermute | solution.py:492
  406.7 82.7 %collective-permute-start.16 = (bf16[384,1536]{1,0:T(8,128)(2,1)}, bf16[384,1536]{1,0:T(8,128)(2,1)}, u32[]{:S(2)}, u32[]{:S(2)}) collective-permute-start(bf16[384,1536]{1,0:T(8,128)(2,1)} %add_convert_fusion.6), channel_id=1, source_target_pairs={{0,4},{2,6},{4,0},{6,2},{1,5},{3,7},{5,1},{7,3},{8,12},{10,14},{12... | collective-permute-start | bytes 3538952 | tf_op jit(solution)/shard_map/ppermute | solution.py:492
  469.9 25.7 %collective-permute-start.26 = (bf16[96,2048]{1,0:T(8,128)(2,1)S(1)}, bf16[96,2048]{1,0:T(8,128)(2,1)S(1)}, u32[]{:S(2)}, u32[]{:S(2)}) collective-permute-start(bf16[96,2048]{1,0:T(8,128)(2,1)S(1)} %get-tuple-element.91), channel_id=1, source_target_pairs={{0,8},{8,16},{16,24},{24,0},{1,9},{9,17},{17,25},{25,1},{2,10},{10... | collective-permute-start | bytes 1179656 | tf_op jit(solution)/shard_map/ppermute | solution.py:591
  471.7 27.0 %collective-permute-start.27 = (bf16[96,2048]{1,0:T(8,128)(2,1)S(1)}, bf16[96,2048]{1,0:T(8,128)(2,1)S(1)}, u32[]{:S(2)}, u32[]{:S(2)}) collective-permute-start(bf16[96,2048]{1,0:T(8,128)(2,1)S(1)} %get-tuple-element.93), channel_id=1, source_target_pairs={{0,16},{8,24},{16,0},{24,8},{1,17},{9,25},{17,1},{25,9},{2,18},{10... | collective-permute-start | bytes 1179656 | tf_op jit(solution)/shard_map/ppermute | solution.py:591
  473.8 24.9 %collective-permute-start.28 = (bf16[96,2048]{1,0:T(8,128)(2,1)S(1)}, bf16[96,2048]{1,0:T(8,128)(2,1)S(1)}, u32[]{:S(2)}, u32[]{:S(2)}) collective-permute-start(bf16[96,2048]{1,0:T(8,128)(2,1)S(1)} %get-tuple-element.92), channel_id=1, source_target_pairs={{0,24},{8,0},{16,8},{24,16},{1,25},{9,1},{17,9},{25,17},{2,26},{10... | collective-permute-start | bytes 1179656 | tf_op jit(solution)/shard_map/ppermute | solution.py:591
  493.1 30.3 %collective-permute-start.18 = (bf16[96,1536]{1,0:T(8,128)(2,1)S(1)}, bf16[96,1536]{1,0:T(8,128)(2,1)S(1)}, u32[]{:S(2)}, u32[]{:S(2)}) collective-permute-start(bf16[96,1536]{1,0:T(8,128)(2,1)S(1)} %get-tuple-element.96), channel_id=1, source_target_pairs={{0,16},{8,24},{16,0},{24,8},{1,17},{9,25},{17,1},{25,9},{2,18},{10... | collective-permute-start | bytes 884744 | tf_op jit(solution)/shard_map/ppermute | solution.py:591
  495.6 27.9 %collective-permute-start.19 = (bf16[96,1536]{1,0:T(8,128)(2,1)S(1)}, bf16[96,1536]{1,0:T(8,128)(2,1)S(1)}, u32[]{:S(2)}, u32[]{:S(2)}) collective-permute-start(bf16[96,1536]{1,0:T(8,128)(2,1)S(1)} %get-tuple-element.95), channel_id=1, source_target_pairs={{0,24},{8,0},{16,8},{24,16},{1,25},{9,1},{17,9},{25,17},{2,26},{10... | collective-permute-start | bytes 884744 | tf_op jit(solution)/shard_map/ppermute | solution.py:591
  (34 other events, 395.7 us)
Sparse Core Ops, SparseCore 0:
  10.8 83.6 all-gather.2
  96.1 118.7 all-gather.4
  253.6 64.0 reduce-scatter.5
  391.3 29.5 reduce-scatter.3
  435.4 36.2 reduce-scatter.7
